TPU v7x, 128 devices: a whole 4x4x4 slice. The times are simulated.
128 devices in a mesh: pipe: 4 (over x), expert: 32 (over z, y, core).
Axes of the slice: x: 4, y: 4, z: 4, core: 2. Of those that a mesh axis runs over, the one named last changes fastest.
Arguments:
- grad_rows: bfloat16 [2, 4, 4096, 3584], P(None, 'pipe', 'expert'), may hold values from -0.29882812 to 0.29882812
- expert_ids: int32 [2, 4, 4096, 8], P(None, 'pipe', 'expert'), may hold values from 0 to 31, all different within a row; in each aligned block of 128 rows (0 to 127, 128 to 255, ..., all dimensions but the last counted through in order) at most 40 rows name the same one
- gate_buckets: int32 [2, 4, 4096, 8], P(None, 'pipe', 'expert'), may hold values from 1 to 64
- saved_hidden: bfloat16 [2, 4, 32, 1280, 1280], P(None, 'pipe', 'expert'), may hold values from -6 to 6
Outputs:
- weight_grad: bfloat16 [4, 32, 1280, 3584], P('pipe', 'expert')
Inputs may be any that keep to these rules, and one draw needn't show every extreme that they name: `expert_ids`: in every direction and rank, each aligned block of 128 tokens names each expert in at most 40 routes and some expert in exactly 40; the 8 ids of a token differ.
All inputs are finite; a program needn't handle non-finite values.
Results may differ from a plain program's by a relative error of at most 0.0058.
Values may be sent and summed in bfloat16 or wider, within the bound.
A program may use at most 128 MiB of HBM per device.

v0:
```python
import jax
import jax.numpy as jnp
from jax import lax
from jax.sharding import PartitionSpec as P


def swapped(shard, axis, distance):
    return lax.ppermute(shard, axis, [(i, i ^ 1 << distance) for i in range(lax.axis_size(axis))])


def build_outbound(token_rows, route_ids, bucket_ids, experts, capacity):
    tok_count, top_count = route_ids.shape
    flat_ids = route_ids.reshape(-1)
    one_hot = (flat_ids[:, None] == jnp.arange(experts, dtype=jnp.int32)[None, :]).astype(jnp.int32)
    earlier = jnp.cumsum(one_hot, axis=0) - one_hot
    position = jnp.sum(earlier * one_hot, axis=1)
    slot_ids = flat_ids * capacity + position
    weighting = bucket_ids.reshape(-1).astype(jnp.float32) / 64.0
    slot_table = (
        slot_ids[:, None] == jnp.arange(experts * capacity, dtype=jnp.int32)[None, :]
    ).astype(jnp.float32)
    slot_table = slot_table * weighting[:, None]
    spread = jnp.sum(slot_table.reshape(tok_count, top_count, experts * capacity), axis=1).astype(
        jnp.bfloat16
    )
    outbound = lax.dot_general(
        spread, token_rows, (((0,), (0,)), ((), ())), preferred_element_type=jnp.float32
    )
    return outbound.astype(jnp.bfloat16).reshape(experts, capacity, token_rows.shape[1])


def slot_product(hidden_rows, inbound):
    width = inbound.shape[-1]
    flat_in = inbound.reshape(-1, width)
    product = lax.dot_general(
        hidden_rows, flat_in, (((0,), (0,)), ((), ())), preferred_element_type=jnp.float32
    )
    return product.astype(jnp.bfloat16)


def on_device(grad_rows, expert_ids, gate_buckets, saved_hidden):
    experts = lax.axis_size("expert")
    capacity = saved_hidden.shape[3] // experts
    token_rows = grad_rows[:, 0]
    route_ids = expert_ids[:, 0]
    bucket_ids = gate_buckets[:, 0]
    hidden_rows = saved_hidden[:, 0, 0]
    bit_count = lax.axis_size("pipe").bit_length() - 1
    local_batch = (token_rows[0], route_ids[0], bucket_ids[0], hidden_rows[0])
    other_rows = token_rows[1]
    other_hidden = hidden_rows[1]
    other_ids = route_ids[1]
    other_buckets = bucket_ids[1]
    batches = [local_batch, (other_rows, other_ids, other_buckets, other_hidden)]
    send_list = [
        build_outbound(batch[0], batch[1], batch[2], experts, capacity) for batch in batches
    ]
    arrived = (
        lax.all_to_all(send_list[0], "expert", split_axis=0, concat_axis=0, tiled=True),
        lax.all_to_all(send_list[1], "expert", split_axis=0, concat_axis=0, tiled=True),
    )
    partials = [slot_product(batches[index][3], arrived[index]) for index in range(2)]
    mirrored = partials[1]
    for bit_index in range(bit_count):
        mirrored = swapped(mirrored, "pipe", bit_index)
    total_grad = partials[0].astype(jnp.float32) + mirrored.astype(jnp.float32)
    return total_grad.astype(jnp.bfloat16)[None, None]


def solution(mesh):
    return jax.shard_map(
        on_device,
        mesh=mesh,
        in_specs=(
            P(None, "pipe", "expert", None),
            P(None, "pipe", "expert", None),
            P(None, "pipe", "expert", None),
            P(None, "pipe", "expert", None, None),
        ),
        out_specs=P("pipe", "expert", None, None),
        check_vma=False,
    )
```

profile of v0, /device:TPU:1, one launch (start us, length us, event | category | flops | bytes accessed | tf_op | source)
XLA Modules:
  0.0 565.7 jit_solution(12384590591861380950)
XLA Ops:
  0.0 0.7 fusion.21
  0.7 0.1 copy.29
  1.0 0.7 multiply_bitcast_fusion.1
  1.7 0.1 copy.26
  1.8 9.0 %reduce-window.16 = s32[32,8,128]{2,1,0:T(8,128)S(1)} reduce-window(s32[32,8,128]{2,1,0:T(8,128)S(1)} %fusion.20, s32[]{:T(128)} %constant.15.clone.1), window={size=1x1x128 pad=0_0x0_0x127_0}, to_apply=%region_4.5 | reduce-window | flops 4161536 | bytes 262148 | tf_op jit(solution)/shard_map/reduce-window.2
  10.9 0.1 copy.24
  11.2 0.1 broadcast_add_fusion
  11.4 1.7 select_reduce_fusion
  13.1 3.7 convolution_convert_fusion.2
  16.9 113.5 %all_to_all.10 = bf16[32,40,3584]{2,1,0:T(8,128)(2,1)S(1)} all-to-all(bf16[32,40,3584]{2,1,0:T(8,128)(2,1)S(1)} %bitcast.83), channel_id=1, replica_groups=mesh['pipe'=4,'expert'=32] {'expert'}, dimensions={0} | all-to-all | bytes 18350080 | tf_op jit(solution)/shard_map/all_to_all | solution.py:60
  130.4 16.4 %fusion.1 = bf16[1280,3584]{0,1:T(8,128)(2,1)} fusion(bf16[1280,3584]{1,0:T(8,128)(2,1)S(1)} %bitcast.84, bf16[2,1,1,1280,1280]{4,3,2,1,0:T(8,128)(2,1)} %param.7), kind=kOutput, calls=%fused_computation.6 | convolution fusion | flops 11748638720 | bytes 21626880 | tf_op jit(solution)/shard_map/dot_general | solution.py:35
  146.8 1.2 collective-permute-start
  148.4 9.0 %reduce-window.14 = s32[32,8,128]{2,1,0:T(8,128)S(1)} reduce-window(s32[32,8,128]{2,1,0:T(8,128)S(1)} %fusion.19, s32[]{:T(128)} %constant.15.clone.1), window={size=1x1x128 pad=0_0x0_0x127_0}, to_apply=%region_0.0 | reduce-window | flops 4161536 | bytes 262148 | tf_op jit(solution)/shard_map/reduce-window
  157.5 0.1 copy.20
  157.7 0.1 broadcast_add_fusion.1
  158.0 1.7 select_reduce_fusion.1
  159.7 6.1 %convolution_convert_fusion.3 = bf16[1280,3584]{1,0:T(8,128)(2,1)} fusion(bf16[2,1,128,3584]{3,2,1,0:T(8,128)(2,1)S(1)} %copy-done, bf16[128,1280]{1,0:T(8,128)(2,1)S(1)} %select_reduce_fusion.1), kind=kOutput, calls=%fused_computation.5 | convolution fusion | flops 1178992640 | bytes 10420224 | tf_op jit(solution)/shard_map/dot_general | solution.py:26
  165.8 5.5 all-to-all-start
  171.2 174.1 %collective-permute-done = bf16[1280,3584]{0,1:T(8,128)(2,1)} collective-permute-done((bf16[1280,3584]{0,1:T(8,128)(2,1)}, bf16[1280,3584]{0,1:T(8,128)(2,1)}, u32[]{:S(2)}, u32[]{:S(2)}) %collective-permute-start) | collective-permute-done | bytes 9175072 | tf_op jit(solution)/shard_map/ppermute | solution.py:8
  345.3 2.8 collective-permute-start.1
  348.1 15.7 %convolution_convert_fusion.1 = bf16[3584,1280]{1,0:T(8,128)(2,1)S(1)} fusion(bf16[1280,3584]{1,0:T(8,128)(2,1)} %bitcast.6, bf16[2,1,1,1280,1280]{4,3,2,1,0:T(8,128)(2,1)} %param.7), kind=kOutput, calls=%fused_computation.3 | convolution fusion | flops 11748638720 | bytes 21626880 | tf_op jit(solution)/shard_map/dot_general | solution.py:35
  363.8 180.7 %collective-permute-done.1 = bf16[1280,3584]{0,1:T(8,128)(2,1)} collective-permute-done((bf16[1280,3584]{0,1:T(8,128)(2,1)}, bf16[1280,3584]{0,1:T(8,128)(2,1)}, u32[]{:S(2)}, u32[]{:S(2)}) %collective-permute-start.1) | collective-permute-done | bytes 9175072 | tf_op jit(solution)/shard_map/ppermute | solution.py:8
  544.5 8.5 %fusion.2 = bf16[1,1,1280,3584]{2,3,1,0:T(8,128)(2,1)} fusion(bf16[1280,3584]{0,1:T(8,128)(2,1)} %collective-permute-done.1, bf16[3584,1280]{1,0:T(8,128)(2,1)S(1)} %convolution_convert_fusion.1), kind=kLoop, calls=%fused_computation.7 | loop fusion | flops 18350080 | bytes 27525120 | tf_op jit(solution)/shard_map/broadcast_in_dim | solution.py:67
  552.9 12.7 %copy.27 = bf16[1,1,1280,3584]{3,2,1,0:T(8,128)(2,1)} copy(bf16[1,1,1280,3584]{2,3,1,0:T(8,128)(2,1)} %fusion.2) | data formatting | bytes 18350080 | tf_op jit(solution)/shard_map/broadcast_in_dim | solution.py:67
  (25 shorter events, 1.3 us)
Async XLA Ops:
  130.4 29.3 %copy-start = (bf16[2,1,128,3584]{3,2,1,0:T(8,128)(2,1)S(1)}, bf16[2,1,128,3584]{3,2,1,0:T(8,128)(2,1)}, u32[]{:S(2)}) copy-start(bf16[2,1,128,3584]{3,2,1,0:T(8,128)(2,1)} %param.4) | copy-start | bytes 5505028
  146.8 198.6 %collective-permute-start = (bf16[1280,3584]{0,1:T(8,128)(2,1)}, bf16[1280,3584]{0,1:T(8,128)(2,1)}, u32[]{:S(2)}, u32[]{:S(2)}) collective-permute-start(bf16[1280,3584]{0,1:T(8,128)(2,1)} %fusion.1), channel_id=1, source_target_pairs={{0,32},{32,0},{64,96},{96,64},{1,33},{33,1},{65,97},{97,65},{2,34}... | collective-permute-start | bytes 27525128 | tf_op jit(solution)/shard_map/ppermute | solution.py:8
  165.8 182.3 %all-to-all-start = ((bf16[32,40,3584]{2,1,0:T(8,128)(2,1)}), bf16[32,40,3584]{2,1,0:T(8,128)(2,1)}, u32[]{:S(2)}, u32[]{:S(2)}) async-start(bf16[32,40,3584]{2,1,0:T(8,128)(2,1)} %bitcast.82), calls=%async_computation | async-start | bytes 18350080 | tf_op jit(solution)/shard_map/all_to_all | solution.py:59
  345.3 199.1 %collective-permute-start.1 = (bf16[1280,3584]{0,1:T(8,128)(2,1)}, bf16[1280,3584]{0,1:T(8,128)(2,1)}, u32[]{:S(2)}, u32[]{:S(2)}) collective-permute-start(bf16[1280,3584]{0,1:T(8,128)(2,1)} %collective-permute-done), channel_id=1, source_target_pairs={{0,64},{32,96},{64,0},{96,32},{1,65},{33,97},{65,1},{97,33},{2,66}... | collective-permute-start | bytes 27525128 | tf_op jit(solution)/shard_map/ppermute | solution.py:8
where the time goes:
time: 567 us; the launch traced here: 566 us
  waiting for transfers between devices  355 us (63%)
  blocking collectives  114 us (20%)
  matrix products  41.9 us (7%)
  other arithmetic  30.9 us (5%)
  local copies, waits for them, and re-layouts  15 us (3%)
  starting transfers between devices  9.42 us (2%)
    ppermute x2, waiting for transfers between devices, swapped(): lax.ppermute(shard, axis, [(i, i ^ 1 << distance) for i in range(lax.axis...  355 us
    all_to_all x1, blocking collectives, on_device(): lax.all_to_all(send_list[1], 'expert', split_axis=0, concat_axis=0, tiled...  114 us
    dot_general x2, matrix products, slot_product(): lax.dot_general(hidden_rows, flat_in, (((0,), (0,)), ((), ())), preferred...  32.1 us
    another operation x6, other arithmetic  18.3 us
    broadcast_in_dim x1, local copies, waits for them, and re-layouts, on_device(): return total_grad.astype(jnp.bfloat16)[None, None]  12.7 us
  transfers between devices with their start and end apart: 3, of which 2 were waited for; matrix products, arithmetic and copies ran while one was open for 6% of the time, Pallas kernels for 0%

commit v1 on v0

v1 whole, which is shorter than its diff:
```python
import jax
import jax.numpy as jnp
from jax import lax
from jax.sharding import PartitionSpec as P


def build_outbound(token_rows, route_ids, bucket_ids, experts, capacity):
    tokens = token_rows.shape[0]
    member = route_ids[:, :, None] == jnp.arange(experts, dtype=jnp.int32)[None, None, :]
    named = jnp.any(member, axis=1)
    weight = jnp.sum(jnp.where(member, bucket_ids[:, :, None], 0), axis=1).astype(jnp.float32) / 64.0
    before = jnp.arange(tokens)[:, None] < jnp.arange(tokens)[None, :]
    rank = lax.dot_general(
        named.astype(jnp.bfloat16), before.astype(jnp.bfloat16), (((0,), (0,)), ((), ())),
        preferred_element_type=jnp.float32,
    )
    rank = jnp.where(named.T, rank, -1.0)
    slots = jnp.arange(capacity, dtype=jnp.float32)
    spread = jnp.where(rank[:, None, :] == slots[None, :, None], weight.T[:, None, :], 0.0)
    spread = spread.astype(jnp.bfloat16).reshape(experts * capacity, tokens)
    outbound = lax.dot_general(
        spread, token_rows, (((1,), (0,)), ((), ())), preferred_element_type=jnp.float32
    )
    return outbound.astype(jnp.bfloat16).reshape(experts, capacity, token_rows.shape[1])


def on_device(grad_rows, expert_ids, gate_buckets, saved_hidden):
    experts = lax.axis_size("expert")
    ranks = lax.axis_size("pipe")
    capacity = saved_hidden.shape[3] // experts
    mirror = [(i, ranks - 1 - i) for i in range(ranks)]

    def mirrored(value):
        return lax.ppermute(value, "pipe", mirror)

    rows = (grad_rows[0, 0], mirrored(grad_rows[1, 0]))
    ids = (expert_ids[0, 0], mirrored(expert_ids[1, 0]))
    buckets = (gate_buckets[0, 0], mirrored(gate_buckets[1, 0]))
    hidden = (saved_hidden[0, 0, 0], mirrored(saved_hidden[1, 0, 0]))
    parts = []
    for index in range(2):
        outbound = build_outbound(rows[index], ids[index], buckets[index], experts, capacity)
        arrived = lax.all_to_all(outbound, "expert", split_axis=0, concat_axis=0, tiled=True)
        parts.append(
            lax.dot_general(
                hidden[index], arrived.reshape(-1, arrived.shape[-1]), (((0,), (0,)), ((), ())),
                preferred_element_type=jnp.float32,
            ).astype(jnp.bfloat16)
        )
    total = parts[0].astype(jnp.float32) + parts[1].astype(jnp.float32)
    return total.astype(jnp.bfloat16)[None, None]


def solution(mesh):
    return jax.shard_map(
        on_device,
        mesh=mesh,
        in_specs=(
            P(None, "pipe", "expert", None),
            P(None, "pipe", "expert", None),
            P(None, "pipe", "expert", None),
            P(None, "pipe", "expert", None, None),
        ),
        out_specs=P("pipe", "expert", None, None),
        check_vma=False,
    )
```

time: 567 us -> 286 us (0.50)
  the two profiles are of different devices: /device:TPU:1 before, /device:TPU:0 now
where the time goes in v1:
time: 286 us; the launch traced here: 285 us
  waiting for transfers between devices  196 us (69%)
  matrix products  50.1 us (18%)
  starting transfers between devices  22.7 us (8%)
  local copies, waits for them, and re-layouts  15.8 us (6%)
    all_to_all x2, waiting for transfers between devices, on_device(): lax.all_to_all(outbound, 'expert', split_axis=0, concat_axis=0, tiled=True)  125 us
    ppermute x4, waiting for transfers between devices, mirrored(): return lax.ppermute(value, 'pipe', mirror)  71.3 us
    dot_general x2, matrix products, on_device(): lax.dot_general(hidden[index], arrived.reshape(-1, arrived.shape[-1]), ((...  36.4 us
    all_to_all x2, starting transfers between devices, on_device(): lax.all_to_all(outbound, 'expert', split_axis=0, concat_axis=0, tiled=True)  13.6 us
    dot_general x2, matrix products, build_outbound(): lax.dot_general(spread, token_rows, (((1,), (0,)), ((), ())), preferred_e...  13.4 us
    broadcast_in_dim x1, local copies, waits for them, and re-layouts, on_device(): return total.astype(jnp.bfloat16)[None, None]  12.7 us
    ppermute x4, starting transfers between devices, mirrored(): return lax.ppermute(value, 'pipe', mirror)  9.09 us
  transfers between devices with their start and end apart: 6, of which 4 were waited for; matrix products, arithmetic and copies ran while one was open for 9% of the time, Pallas kernels for 0%

profile of v1, /device:TPU:0, one launch (start us, length us, event | category | flops | bytes accessed | tf_op | source)
XLA Modules:
  0.0 285.1 jit_solution(3248186818338742714)
XLA Ops:
  0.0 0.7 slice_bitcast_fusion.4
  0.8 0.1 convolution_select_fusion
  0.9 0.1 select_convert_fusion
  1.0 7.2 %convolution_convert_fusion.3 = bf16[1280,3584]{1,0:T(8,128)(2,1)} fusion(bf16[1280,128]{1,0:T(8,128)(2,1)S(1)} %bitcast.53, bf16[2,1,128,3584]{3,2,1,0:T(8,128)(2,1)} %param.4), kind=kOutput, calls=%fused_computation.4 | convolution fusion | flops 1178992640 | bytes 10420224 | tf_op jit(solution)/shard_map/dot_general | solution.py:21
  8.3 8.7 %all-to-all-start = ((bf16[32,40,3584]{2,1,0:T(8,128)(2,1)}), bf16[32,40,3584]{2,1,0:T(8,128)(2,1)}, u32[]{:S(2)}, u32[]{:S(2)}) async-start(bf16[32,40,3584]{2,1,0:T(8,128)(2,1)} %bitcast.51), calls=%async_computation | async-start | bytes 18350080 | tf_op jit(solution)/shard_map/all_to_all | solution.py:43
  16.9 0.1 slice_bitcast_fusion.1
  17.0 2.8 collective-permute-start.2
  19.8 0.5 collective-permute-start
  20.3 2.8 collective-permute-start.1
  23.1 0.1 eq.82
  23.2 17.7 %collective-permute-done = s32[128,8]{0,1:T(8,128)S(1)} collective-permute-done((s32[128,8]{0,1:T(8,128)S(1)}, s32[128,8]{0,1:T(8,128)S(1)}, u32[]{:S(2)}, u32[]{:S(2)}) %collective-permute-start) | collective-permute-done | bytes 4128 | tf_op jit(solution)/shard_map/ppermute | solution.py:34
  40.9 0.0 collective-permute-done.1
  41.0 0.1 bitcast_select_fusion.1
  41.1 0.2 fusion.5
  41.4 6.2 %convolution_convert_fusion.2 = bf16[1280,3584]{1,0:T(8,128)(2,1)} fusion(bf16[1280,128]{1,0:T(8,128)(2,1)S(1)} %fusion.5, bf16[128,3584]{1,0:T(8,128)(2,1)S(1)} %collective-permute-done.2), kind=kOutput, calls=%fused_computation.3 | convolution fusion | flops 1178992640 | bytes 10420224 | tf_op jit(solution)/shard_map/dot_general | solution.py:21
  47.5 85.3 %all-to-all-done = bf16[32,40,3584]{2,1,0:T(8,128)(2,1)} async-done(((bf16[32,40,3584]{2,1,0:T(8,128)(2,1)}), bf16[32,40,3584]{2,1,0:T(8,128)(2,1)}, u32[]{:S(2)}, u32[]{:S(2)}) %all-to-all-start) | async-done | bytes 9175072 | tf_op jit(solution)/shard_map/all_to_all | solution.py:43
  132.9 5.0 %all-to-all-start.1 = ((bf16[32,40,3584]{2,1,0:T(8,128)(2,1)}), bf16[32,40,3584]{2,1,0:T(8,128)(2,1)}, u32[]{:S(2)}, u32[]{:S(2)}) async-start(bf16[32,40,3584]{2,1,0:T(8,128)(2,1)} %bitcast.52), calls=%async_computation.1 | async-start | bytes 18350080 | tf_op jit(solution)/shard_map/all_to_all | solution.py:43
  137.8 2.1 slice_bitcast_fusion
  140.0 3.0 %collective-permute-start.3 = (bf16[1280,1280]{1,0:T(8,128)(2,1)S(1)}, bf16[1280,1280]{1,0:T(8,128)(2,1)S(1)}, u32[]{:S(2)}, u32[]{:S(2)}) collective-permute-start(bf16[1280,1280]{1,0:T(8,128)(2,1)S(1)} %slice_bitcast_fusion), channel_id=1, source_target_pairs={{0,96},{32,64},{64,32},{96,0},{1,97},{33,65},{65,33},{97,1},{2,98}... | collective-permute-start | bytes 9830408 | tf_op jit(solution)/shard_map/ppermute | solution.py:34
  143.0 17.8 %convolution_convert_fusion.1 = bf16[3584,1280]{1,0:T(8,128)(2,1)} fusion(bf16[1280,3584]{1,0:T(8,128)(2,1)} %bitcast.7, bf16[2,1,1,1280,1280]{4,3,2,1,0:T(8,128)(2,1)} %param.7), kind=kOutput, calls=%fused_computation.2 | convolution fusion | flops 11748638720 | bytes 21626880 | tf_op jit(solution)/shard_map/dot_general | solution.py:45
  160.8 53.5 %collective-permute-done.3 = bf16[1280,1280]{1,0:T(8,128)(2,1)S(1)} collective-permute-done((bf16[1280,1280]{1,0:T(8,128)(2,1)S(1)}, bf16[1280,1280]{1,0:T(8,128)(2,1)S(1)}, u32[]{:S(2)}, u32[]{:S(2)}) %collective-permute-start.3) | collective-permute-done | bytes 3276832 | tf_op jit(solution)/shard_map/ppermute | solution.py:34
  214.4 39.4 %all-to-all-done.1 = bf16[32,40,3584]{2,1,0:T(8,128)(2,1)} async-done(((bf16[32,40,3584]{2,1,0:T(8,128)(2,1)}), bf16[32,40,3584]{2,1,0:T(8,128)(2,1)}, u32[]{:S(2)}, u32[]{:S(2)}) %all-to-all-start.1) | async-done | bytes 9175072 | tf_op jit(solution)/shard_map/all_to_all | solution.py:43
  253.7 18.6 %fusion = bf16[1,1,1280,3584]{2,3,1,0:T(8,128)(2,1)} fusion(bf16[1280,3584]{1,0:T(8,128)(2,1)} %bitcast.17, bf16[1280,1280]{1,0:T(8,128)(2,1)S(1)} %collective-permute-done.3, bf16[3584,1280]{1,0:T(8,128)(2,1)} %convolution_convert_fusion.1), kind=kOutput, calls=%fused_computation.5 | convolution fusion | flops 11766988800 | bytes 30801920 | tf_op jit(solution)/shard_map/dot_general | solution.py:45
  272.3 12.7 %copy.10 = bf16[1,1,1280,3584]{3,2,1,0:T(8,128)(2,1)} copy(bf16[1,1,1280,3584]{2,3,1,0:T(8,128)(2,1)} %fusion) | data formatting | bytes 18350080 | tf_op jit(solution)/shard_map/broadcast_in_dim | solution.py:51
  (10 shorter events, 0.1 us)
Async XLA Ops:
  8.3 8.7 %copy-start = (bf16[2,1,128,3584]{3,2,1,0:T(8,128)(2,1)S(1)}, bf16[2,1,128,3584]{3,2,1,0:T(8,128)(2,1)}, u32[]{:S(2)}) copy-start(bf16[2,1,128,3584]{3,2,1,0:T(8,128)(2,1)} %param.4) | copy-start | bytes 5505028
  8.3 124.6 %all-to-all-start = ((bf16[32,40,3584]{2,1,0:T(8,128)(2,1)}), bf16[32,40,3584]{2,1,0:T(8,128)(2,1)}, u32[]{:S(2)}, u32[]{:S(2)}) async-start(bf16[32,40,3584]{2,1,0:T(8,128)(2,1)} %bitcast.51), calls=%async_computation | async-start | bytes 18350080 | tf_op jit(solution)/shard_map/all_to_all | solution.py:43
  17.0 24.3 %collective-permute-start.2 = (bf16[128,3584]{1,0:T(8,128)(2,1)S(1)}, bf16[128,3584]{1,0:T(8,128)(2,1)S(1)}, u32[]{:S(2)}, u32[]{:S(2)}) collective-permute-start(bf16[128,3584]{1,0:T(8,128)(2,1)S(1)} %slice_bitcast_fusion.1), channel_id=1, source_target_pairs={{0,96},{32,64},{64,32},{96,0},{1,97},{33,65},{65,33},{97,1},{2,98}... | collective-permute-start | bytes 2752520 | tf_op jit(solution)/shard_map/ppermute | solution.py:34
  19.8 21.0 %collective-permute-start = (s32[128,8]{0,1:T(8,128)S(1)}, s32[128,8]{0,1:T(8,128)S(1)}, u32[]{:S(2)}, u32[]{:S(2)}) collective-permute-start(s32[128,8]{0,1:T(8,128)S(1)} %get-tuple-element.9), channel_id=1, source_target_pairs={{0,96},{32,64},{64,32},{96,0},{1,97},{33,65},{65,33},{97,1},{2,98}... | collective-permute-start | bytes 12296 | tf_op jit(solution)/shard_map/ppermute | solution.py:34
  20.3 20.6 %collective-permute-start.1 = (s32[128,8]{0,1:T(8,128)S(1)}, s32[128,8]{0,1:T(8,128)S(1)}, u32[]{:S(2)}, u32[]{:S(2)}) collective-permute-start(s32[128,8]{0,1:T(8,128)S(1)} %get-tuple-element.8), channel_id=1, source_target_pairs={{0,96},{32,64},{64,32},{96,0},{1,97},{33,65},{65,33},{97,1},{2,98}... | collective-permute-start | bytes 12296 | tf_op jit(solution)/shard_map/ppermute | solution.py:34
  132.9 120.9 %all-to-all-start.1 = ((bf16[32,40,3584]{2,1,0:T(8,128)(2,1)}), bf16[32,40,3584]{2,1,0:T(8,128)(2,1)}, u32[]{:S(2)}, u32[]{:S(2)}) async-start(bf16[32,40,3584]{2,1,0:T(8,128)(2,1)} %bitcast.52), calls=%async_computation.1 | async-start | bytes 18350080 | tf_op jit(solution)/shard_map/all_to_all | solution.py:43
  140.0 74.4 %collective-permute-start.3 = (bf16[1280,1280]{1,0:T(8,128)(2,1)S(1)}, bf16[1280,1280]{1,0:T(8,128)(2,1)S(1)}, u32[]{:S(2)}, u32[]{:S(2)}) collective-permute-start(bf16[1280,1280]{1,0:T(8,128)(2,1)S(1)} %slice_bitcast_fusion), channel_id=1, source_target_pairs={{0,96},{32,64},{64,32},{96,0},{1,97},{33,65},{65,33},{97,1},{2,98}... | collective-permute-start | bytes 9830408 | tf_op jit(solution)/shard_map/ppermute | solution.py:34

commit v2 on v1

v2 whole, which is shorter than its diff:
```python
import functools

import jax
import jax.numpy as jnp
from jax import lax
from jax.experimental import pallas as pl
from jax.experimental.pallas import tpu as pltpu
from jax.sharding import PartitionSpec as P

MESH = pl.DeviceIdType.MESH
SIDE = 4
CORES = 2
LANES = 128
WIDE = 2 * LANES
TRACKS = 2
BF = jnp.bfloat16
F32 = jnp.float32


def wrap(i):
    return lax.rem(i + 2 * SIDE, SIDE)


def kernel(ranks, cap, tok_ref, ids_ref, gate_ref, hid_ref, out_ref,
           src, ring, pair, tiles, hid_t, hid_out, stage, select, own_tab, tab, tabs,
           to_far, to_sib, done,
           src_sem, x_sem, xt_sem, xh_sem, xsend_sem, stage_sem,
           ring_sem, own_sem, ring_send, pair_sem, pair_send,
           tab_sem, tab_own_sem, tab_send, tab_pair_sem, tab_pair_send,
           tile_sem, far_send, sib_send, done_sem):
    tokens, width = tok_ref.shape[1], tok_ref.shape[2]
    slots, units = hid_ref.shape[1], hid_ref.shape[2]
    half = width // CORES
    chunks = half // WIDE
    steps = 2 * chunks
    both = CORES * cap
    piece = units // SIDE

    rank = lax.axis_index("pipe")
    expert = lax.axis_index("expert")
    c = lax.rem(expert, CORES)
    y = lax.rem(expert // CORES, SIDE)
    z = expert // (CORES * SIDE)
    mine_a = (1 - c) * z + c * y
    mine_b = (1 - c) * y + c * z
    step_a = lax.rem(mine_b, 2)
    near = wrap(mine_b + 1 - 2 * step_a)
    far = wrap(mine_b - 1 + 2 * step_a)

    def at(z_, y_, core):
        return {"pipe": rank, "expert": (z_ * SIDE + y_) * CORES + core}

    def at_ab(a_, b_, core):
        return at((1 - c) * a_ + c * b_, (1 - c) * b_ + c * a_, core)

    def expert_ab(a_, b_, core):
        return (((1 - c) * a_ + c * b_) * SIDE + (1 - c) * b_ + c * a_) * CORES + core

    sibling = at(z, y, 1 - c)
    mirror = {"pipe": ranks - 1 - rank, "expert": expert}

    def send(s_ref, d_ref, s_sem, r_sem, dev):
        pltpu.make_async_remote_copy(
            src_ref=s_ref, dst_ref=d_ref, send_sem=s_sem, recv_sem=r_sem,
            device_id=dev, device_id_type=MESH).start()

    def await_bytes(ref, sem):
        pltpu.make_async_copy(ref, ref, sem).wait()

    first = pltpu.make_async_copy(tok_ref.at[0], src.at[0], src_sem)
    first.start()

    def load_hidden(n):
        d, part = (1, n) if n < slots // WIDE else (0, n - slots // WIDE)
        return pltpu.make_async_copy(
            hid_ref.at[d, pl.ds(part * WIDE, WIDE)], stage.at[n % 2], stage_sem.at[n % 2])

    load_hidden(0).start()
    load_hidden(1).start()

    barrier = pltpu.get_barrier_semaphore()
    friends = [sibling, mirror]
    for core in range(CORES):
        for turn in (1, SIDE - 1):
            friends.append(at(wrap(z + turn), y, core))
            friends.append(at(z, wrap(y + turn), core))
    for friend in friends:
        pl.semaphore_signal(barrier, inc=1, device_id=friend, device_id_type=MESH)
    pl.semaphore_wait(barrier, len(friends))

    for k in range(chunks):
        for h in range(CORES):
            cols = pl.ds(h * half + k * WIDE, WIDE)
            send(tok_ref.at[1, :, cols], src.at[1, :, cols], xsend_sem.at[0], x_sem.at[k], mirror)

    e_row = lax.broadcasted_iota(jnp.int32, (SIDE * SIDE * CORES, tokens), 0)
    before = (lax.broadcasted_iota(jnp.int32, (tokens, tokens), 0)
              < lax.broadcasted_iota(jnp.int32, (tokens, tokens), 1)).astype(F32).astype(BF)
    for d in range(2):
        ids = ids_ref[d]
        top = ids.shape[0]
        named = jnp.zeros(e_row.shape, F32)
        for j in range(top):
            named += jnp.where(e_row == ids[j:j + 1, :], 1.0, 0.0)
        earlier = jnp.dot(named.astype(BF), before, preferred_element_type=F32)
        spots = [jnp.sum(jnp.where(e_row == ids[j:j + 1, :], earlier, 0.0), axis=0, keepdims=True)
                 for j in range(top)]
        into = tab.at[0] if d == 0 else own_tab
        into[0] = ids.astype(F32)
        into[1] = jnp.concatenate(spots, axis=0)
        into[2] = gate_ref[d].astype(F32) / 64.0

    first.wait()

    def ring_out(source, dest, sems, send_sem, own, cols_of):
        for h in range(CORES):
            a_h = z if h == 0 else y
            for turn in (1, -1):
                dev = at(wrap(z + turn), y, 0) if h == 0 else at(z, wrap(y + turn), 1)
                which = 2 * c if turn == 1 else 2 - c
                send(cols_of(source, h), dest.at[a_h * CORES + c], send_sem, sems.at[which], dev)
        sib_a = c * z + (1 - c) * y
        send(cols_of(source, 1 - c), dest.at[sib_a * CORES + c], send_sem, sems.at[2], sibling)
        pltpu.make_async_copy(cols_of(source, c), dest.at[mine_a * CORES + c], own).start()

    def ring_on(dest, sems, send_sem):
        for turn, core in ((1, 0), (-1, 1)):
            part = dest.at[wrap(mine_a - turn) * CORES + core]
            await_bytes(part, sems.at[core])
            send(part, part, send_sem, sems.at[2], at_ab(wrap(mine_a + turn), mine_b, c))

    def step_cols(k):
        return lambda ref, h: ref.at[:, pl.ds(pl.multiple_of(h * half + k * WIDE, LANES), WIDE)]

    def stage_a(s):
        d, k = s // chunks, lax.rem(s, chunks)

        @pl.when(d == 1)
        def _():
            await_bytes(src.at[1, :, pl.ds(0, 2 * WIDE)], x_sem.at[k])

        @pl.when(k == 0)
        def _():
            @pl.when(d == 1)
            def _():
                await_bytes(tab.at[1], xt_sem)
            ring_out(tab.at[d], tabs.at[d, 0], tab_sem.at[d], tab_send.at[d], tab_own_sem.at[d],
                     lambda ref, h: ref)

        ring_out(src.at[d], ring.at[s], ring_sem.at[s], ring_send.at[s], own_sem.at[s], step_cols(k))

    def stage_b(s):
        d, k = s // chunks, lax.rem(s, chunks)

        @pl.when(k == 0)
        def _():
            ring_on(tabs.at[d, 0], tab_sem.at[d], tab_send.at[d])

        ring_on(ring.at[s], ring_sem.at[s], ring_send.at[s])

    def stage_c(s):
        d, k = s // chunks, lax.rem(s, chunks)

        @pl.when(k == 0)
        def _():
            await_bytes(tabs.at[d, 0, pl.ds(0, 5)], tab_sem.at[d, 2])
            await_bytes(tabs.at[d, 0, 0], tab_own_sem.at[d])
            for p, friend in ((0, near), (1, far)):
                send(tabs.at[d, 0], tabs.at[d, 1 + p], tab_pair_send.at[d], tab_pair_sem.at[d],
                     at_ab(mine_a, friend, c))

        await_bytes(ring.at[s, pl.ds(0, 5)], ring_sem.at[s, 2])
        await_bytes(ring.at[s, 0], own_sem.at[s])
        for p, friend in ((0, near), (1, far)):
            send(ring.at[s, :, :, pl.ds(p * LANES, LANES)], pair.at[s, p], pair_send.at[s],
                 pair_sem.at[s], at_ab(mine_a, friend, c))

    row = lax.broadcasted_iota(jnp.int32, (both, CORES * tokens), 0)
    lane = lax.broadcasted_iota(jnp.int32, (both, CORES * tokens), 1)
    target = jnp.where((row < cap) == (lane < tokens), jnp.where(row < cap, row, row - cap), -2).astype(F32)

    def select_rows(d, where_, a_, e):
        found = []
        for core in range(CORES):
            t = tabs.at[d, where_, a_ * CORES + core]
            hit = t[0] == e.astype(F32)
            spot = jnp.sum(jnp.where(hit, t[1] + 1.0, 0.0), axis=0, keepdims=True) - 1.0
            weight = jnp.sum(jnp.where(hit, t[2], 0.0), axis=0, keepdims=True)
            found.append((spot, weight))
        spot = jnp.concatenate([f[0] for f in found], axis=1)
        weight = jnp.concatenate([f[1] for f in found], axis=1)
        return jnp.where(spot == target, weight, 0.0).astype(BF)

    own2 = [(mine_b, c), (mine_b, 1 - c)]
    near2 = [(near, 0), (near, 1)]
    far2 = [(far, 0), (far, 1)]
    plan = [(0, x) for x in near2 + own2 + far2] + [(1, x) for x in own2 + far2] + [(2, x) for x in near2 + own2]

    def build_select(d):
        @pl.loop(0, SIDE)
        def _(a_):
            for n, (where_, (b_, core)) in enumerate(plan):
                select[a_, pl.ds(n * both, both), :] = select_rows(d, where_, a_, expert_ab(mine_a, b_, core))

    lead = {(0, 0): 2, (0, 1): 6, (1, 0): 0, (1, 1): 10}

    def stage_d(s):
        d, k = s // chunks, lax.rem(s, chunks)
        track = lax.rem(s, TRACKS)

        @pl.when(k == 0)
        def _():
            await_bytes(tabs.at[d, pl.ds(1, 2)], tab_pair_sem.at[d])
            build_select(d)

        @pl.when(s >= TRACKS)
        def _():
            await_bytes(to_far.at[track], far_send.at[track])
            await_bytes(to_sib.at[track], sib_send.at[track])

        await_bytes(ring.at[s], pair_sem.at[s])
        for p in range(2):
            friend = near if p == 0 else far
            for b_at in range(2):
                b_ = mine_b if b_at == 0 else friend
                start = lead[(p, b_at)] * both

                @pl.loop(0, SIDE)
                def _(a_):
                    if b_at == 0:
                        rows = ring[s, pl.ds(a_ * CORES, CORES), :, p * LANES:(p + 1) * LANES]
                    else:
                        rows = pair[s, p, pl.ds(a_ * CORES, CORES)]
                    rows = rows.reshape(CORES * tokens, LANES)
                    got = jnp.dot(select[a_, pl.ds(start, 4 * both), :], rows,
                                  preferred_element_type=F32).astype(BF)
                    own_at = 0 if p == 0 else 2 * both
                    far_at = 2 * both if p == 0 else 0
                    z_, y_ = (1 - c) * a_ + c * b_, (1 - c) * b_ + c * a_
                    tiles[1 + s * CORES + c, z_, y_, :, p * LANES:(p + 1) * LANES] = got[own_at:own_at + both]
                    to_sib[track, p, b_at, a_] = got[own_at + both:own_at + 2 * both]
                    for core in range(CORES):
                        to_far[track, p, core, b_at, a_] = got[far_at + core * both:far_at + (core + 1) * both]

        for h in range(CORES):
            @pl.when(c == h)
            def _():
                into = tiles.at[1 + s * CORES + h]
                for p in range(2):
                    cols = pl.ds(p * LANES, LANES)
                    friend = near if p == 0 else far
                    other = far if p == 0 else near
                    for b_at in range(2):
                        b_ = mine_b if b_at == 0 else friend
                        part = into.at[:, b_, :, cols] if h == 0 else into.at[b_, :, :, cols]
                        for core in range(CORES):
                            send(to_far.at[track, p, core, b_at], part, far_send.at[track],
                                 tile_sem.at[s * CORES + h], at_ab(mine_a, other, core))
                        send(to_sib.at[track, p, b_at], part, sib_send.at[track],
                             tile_sem.at[s * CORES + h], sibling)

    def stage_e(s):
        d, k = s // chunks, lax.rem(s, chunks)
        await_bytes(tiles.at[0, pl.ds(0, 2)], tile_sem.at[s * CORES + c])
        await_bytes(tiles.at[0], tile_sem.at[s * CORES + 1 - c])

        @pl.when(d == 0)
        def _():
            @pl.loop(0, CORES)
            def _(h):
                t = s * CORES + h

                @pl.loop(0, SIDE)
                def _(f):
                    got = jnp.dot(hid_t[0, pl.ds(f * piece, piece), :], tiles[t + 1].reshape(slots, WIDE),
                                  preferred_element_type=F32)
                    tiles[t, f] = got.astype(BF).reshape(SIDE, both, WIDE)

        @pl.when(s == chunks)
        def _():
            await_bytes(hid_t.at[1], xh_sem)

        @pl.when(d == 1)
        def _():
            @pl.loop(0, CORES)
            def _(h):
                t = s * CORES + h

                @pl.when(s > chunks)
                def _():
                    await_bytes(done.at[h], done_sem.at[h])

                @pl.loop(0, SIDE)
                def _(f):
                    got = jnp.dot(hid_t[1, pl.ds(f * piece, piece), :], tiles[t + 1].reshape(slots, WIDE),
                                  preferred_element_type=F32)
                    prior = tiles[t - chunks * CORES, f].reshape(piece, WIDE)
                    done[h, pl.ds(f * piece, piece), :] = (got + prior.astype(F32)).astype(BF)

                pltpu.make_async_copy(
                    done.at[h],
                    out_ref.at[:, pl.ds(pl.multiple_of(h * half + k * WIDE, LANES), WIDE)],
                    done_sem.at[h]).start()

    def transpose_hidden():
        parts = slots // WIDE
        for n in range(2 * parts):
            load_hidden(n).wait()
            into = hid_out if n < parts else hid_t.at[0]
            part = n % parts

            @pl.loop(0, units // WIDE)
            def _(f):
                at_f = pl.multiple_of(f * WIDE, WIDE)
                into[pl.ds(at_f, WIDE), part * WIDE:(part + 1) * WIDE] = stage[n % 2, :, pl.ds(at_f, WIDE)].T

            if n + 2 < 2 * parts:
                load_hidden(n + 2).start()

    stage_a(jnp.int32(0))
    send(own_tab, tab.at[1], xsend_sem.at[1], xt_sem, mirror)
    stage_a(jnp.int32(1))
    stage_b(jnp.int32(0))
    transpose_hidden()
    send(hid_out, hid_t.at[1], xsend_sem.at[2], xh_sem, mirror)

    def turn(i, carry):
        for lag, work in ((0, stage_a), (1, stage_b), (2, stage_c), (3, stage_d), (4, stage_e)):
            skip = {0: 2, 1: 1}.get(lag, 0)

            @pl.when((i - lag >= skip) & (i - lag < steps))
            def _():
                work(i - lag)
        return carry

    lax.fori_loop(2, steps + 4, turn, 0)

    for h in range(CORES):
        await_bytes(done.at[h], done_sem.at[h])
    for track in range(TRACKS):
        await_bytes(to_far.at[track], far_send.at[track])
        await_bytes(to_sib.at[track], sib_send.at[track])
    await_bytes(src.at[1], xsend_sem.at[0])
    await_bytes(own_tab, xsend_sem.at[1])
    await_bytes(hid_out, xsend_sem.at[2])

    @pl.loop(0, steps)
    def _(s):
        await_bytes(ring.at[s, pl.ds(0, 7)], ring_send.at[s])
        await_bytes(ring.at[s], pair_send.at[s])

    for d in range(2):
        await_bytes(tabs.at[d, 0, pl.ds(0, 7)], tab_send.at[d])
        await_bytes(tabs.at[d, pl.ds(1, 2)], tab_pair_send.at[d])


def on_device(ranks, grad_rows, expert_ids, gate_buckets, saved_hidden):
    tok, hid = grad_rows[:, 0], saved_hidden[:, 0, 0]
    ids = expert_ids[:, 0].transpose(0, 2, 1)
    gates = gate_buckets[:, 0].transpose(0, 2, 1)
    tokens, width = tok.shape[1:]
    top = ids.shape[1]
    slots, units = hid.shape[1:]
    cap = slots // (SIDE * SIDE * CORES)
    both = CORES * cap
    steps = width // WIDE
    dma = pltpu.SemaphoreType.DMA
    result = pl.pallas_call(
        functools.partial(kernel, ranks, cap),
        out_shape=jax.ShapeDtypeStruct((units, width), BF),
        in_specs=[
            pl.BlockSpec(memory_space=pl.ANY),
            pl.BlockSpec(memory_space=pltpu.VMEM),
            pl.BlockSpec(memory_space=pltpu.VMEM),
            pl.BlockSpec(memory_space=pl.ANY),
        ],
        out_specs=pl.BlockSpec(memory_space=pl.ANY),
        scratch_shapes=[
            pltpu.VMEM((2, tokens, width), BF),
            pltpu.VMEM((steps, SIDE * CORES, tokens, WIDE), BF),
            pltpu.VMEM((steps, 2, SIDE * CORES, tokens, LANES), BF),
            pltpu.VMEM((1 + steps * CORES, SIDE, SIDE, both, WIDE), BF),
            pltpu.VMEM((2, units, slots), BF),
            pltpu.VMEM((units, slots), BF),
            pltpu.VMEM((2, WIDE, units), BF),
            pltpu.VMEM((SIDE, 14 * both, CORES * tokens), BF),
            pltpu.VMEM((3, top, tokens), F32),
            pltpu.VMEM((2, 3, top, tokens), F32),
            pltpu.VMEM((2, 3, SIDE * CORES, 3, top, tokens), F32),
            pltpu.VMEM((TRACKS, 2, CORES, 2, SIDE, both, LANES), BF),
            pltpu.VMEM((TRACKS, 2, 2, SIDE, both, LANES), BF),
            pltpu.VMEM((CORES, units, WIDE), BF),
            dma, dma((steps // 2,)), dma, dma, dma((3,)), dma((2,)),
            dma((steps, 3)), dma((steps,)), dma((steps,)), dma((steps,)), dma((steps,)),
            dma((2, 3)), dma((2,)), dma((2,)), dma((2,)), dma((2,)),
            dma((steps * CORES,)), dma((TRACKS,)), dma((TRACKS,)), dma((2,)),
        ],
        compiler_params=pltpu.CompilerParams(
            collective_id=0, has_side_effects=True, vmem_limit_bytes=66 * 1024 * 1000),
    )(tok, ids, gates, hid)
    return result[None, None]


def solution(mesh):
    return jax.shard_map(
        functools.partial(on_device, mesh.shape["pipe"]),
        mesh=mesh,
        in_specs=(
            P(None, "pipe", "expert", None),
            P(None, "pipe", "expert", None),
            P(None, "pipe", "expert", None),
            P(None, "pipe", "expert", None, None),
        ),
        out_specs=P("pipe", "expert", None, None),
        check_vma=False,
    )
```

time: 286 us -> 157 us (0.55)
  the two profiles are of different devices: /device:TPU:0 before, /device:TPU:1 now
where the time goes in v2:
time: 157 us
  Pallas kernels  149 us (95%)
  local copies, waits for them, and re-layouts  7.85 us (5%)
    pallas_call x1, Pallas kernels, on_device(): pl.pallas_call(functools.partial(kernel, ranks, cap), out_shape=jax.Shape...  149 us
    unnamed x1, local copies, waits for them, and re-layouts  7.85 us

profile of v2, /device:TPU:1, one launch (start us, length us, event | category | flops | bytes accessed | tf_op | source)
XLA Modules:
  0.0 156.8 jit_solution(1540786847988711430)
XLA Ops:
  0.0 148.9 %shard_map.46 = bf16[1280,3584]{1,0:T(8,128)(2,1)} custom-call(bf16[2,128,3584]{2,1,0:T(8,128)(2,1)} %bitcast.11, s32[2,8,128]{2,1,0:T(8,128)} %bitcast.12, s32[2,8,128]{2,1,0:T(8,128)} %bitcast.13, bf16[2,1280,1280]{2,1,0:T(8,128)(2,1)} %bitcast.10), custom_call_target="tpu_custom_call" | custom-call | tf_op jit(solution)/shard_map/pallas_call | solution.py:368
  148.9 7.9 %copy.6 = bf16[1,1,1280,3584]{3,2,1,0:T(8,128)(2,1)} copy(bf16[1,1,1280,3584]{3,2,1,0:T(8,128)(2,1)} %bitcast.9) | data formatting | bytes 18350080

commit v3 on v2

--- a/solution.py
+++ b/solution.py
@@ -12,7 +12,9 @@
 CORES = 2
 LANES = 128
 WIDE = 2 * LANES
-TRACKS = 2
+TRACKS = 3
+LAGS = ((0, 3, 0), (1, 2, 1), (2, 1, 2), (4, 0, 3), (6, 0, 4))
+VLIM = 50 * 1024 * 1024
 BF = jnp.bfloat16
 F32 = jnp.float32
 
@@ -21,13 +23,13 @@
     return lax.rem(i + 2 * SIDE, SIDE)
 
 
-def kernel(ranks, cap, tok_ref, ids_ref, gate_ref, hid_ref, out_ref,
+def kernel(ranks, cap, tok_ref, ids_ref, gate_ref, hid_ref, total,
            src, ring, pair, tiles, hid_t, hid_out, stage, select, own_tab, tab, tabs,
-           to_far, to_sib, done,
+           to_far, to_sib,
            src_sem, x_sem, xt_sem, xh_sem, xsend_sem, stage_sem,
            ring_sem, own_sem, ring_send, pair_sem, pair_send,
            tab_sem, tab_own_sem, tab_send, tab_pair_sem, tab_pair_send,
-           tile_sem, far_send, sib_send, done_sem):
+           tile_sem, far_send, sib_send):
     tokens, width = tok_ref.shape[1], tok_ref.shape[2]
     slots, units = hid_ref.shape[1], hid_ref.shape[2]
     half = width // CORES
@@ -106,9 +108,8 @@
         spots = [jnp.sum(jnp.where(e_row == ids[j:j + 1, :], earlier, 0.0), axis=0, keepdims=True)
                  for j in range(top)]
         into = tab.at[0] if d == 0 else own_tab
-        into[0] = ids.astype(F32)
-        into[1] = jnp.concatenate(spots, axis=0)
-        into[2] = gate_ref[d].astype(F32) / 64.0
+        into[0] = ids.astype(F32) * cap + jnp.concatenate(spots, axis=0)
+        into[1] = gate_ref[d].astype(F32) / 64.0
 
     first.wait()
 
@@ -183,9 +184,10 @@
         found = []
         for core in range(CORES):
             t = tabs.at[d, where_, a_ * CORES + core]
-            hit = t[0] == e.astype(F32)
-            spot = jnp.sum(jnp.where(hit, t[1] + 1.0, 0.0), axis=0, keepdims=True) - 1.0
-            weight = jnp.sum(jnp.where(hit, t[2], 0.0), axis=0, keepdims=True)
+            local = t[0] - (e * cap).astype(F32)
+            hit = (local >= 0.0) & (local < cap)
+            spot = jnp.sum(jnp.where(hit, local + 1.0, 0.0), axis=0, keepdims=True) - 1.0
+            weight = jnp.sum(jnp.where(hit, t[1], 0.0), axis=0, keepdims=True)
             found.append((spot, weight))
         spot = jnp.concatenate([f[0] for f in found], axis=1)
         weight = jnp.concatenate([f[1] for f in found], axis=1)
@@ -237,7 +239,7 @@
                     own_at = 0 if p == 0 else 2 * both
                     far_at = 2 * both if p == 0 else 0
                     z_, y_ = (1 - c) * a_ + c * b_, (1 - c) * b_ + c * a_
-                    tiles[1 + s * CORES + c, z_, y_, :, p * LANES:(p + 1) * LANES] = got[own_at:own_at + both]
+                    tiles[s * CORES + c, z_, y_, :, p * LANES:(p + 1) * LANES] = got[own_at:own_at + both]
                     to_sib[track, p, b_at, a_] = got[own_at + both:own_at + 2 * both]
                     for core in range(CORES):
                         to_far[track, p, core, b_at, a_] = got[far_at + core * both:far_at + (core + 1) * both]
@@ -245,7 +247,7 @@
         for h in range(CORES):
             @pl.when(c == h)
             def _():
-                into = tiles.at[1 + s * CORES + h]
+                into = tiles.at[s * CORES + h]
                 for p in range(2):
                     cols = pl.ds(p * LANES, LANES)
                     friend = near if p == 0 else far
@@ -264,47 +266,33 @@
         await_bytes(tiles.at[0, pl.ds(0, 2)], tile_sem.at[s * CORES + c])
         await_bytes(tiles.at[0], tile_sem.at[s * CORES + 1 - c])
 
-        @pl.when(d == 0)
-        def _():
+        @pl.when(s == chunks)
+        def _():
+            await_bytes(hid_t.at[1], xh_sem)
+
+        def add_product(dest, prior):
             @pl.loop(0, CORES)
             def _(h):
-                t = s * CORES + h
-
                 @pl.loop(0, SIDE)
                 def _(f):
-                    got = jnp.dot(hid_t[0, pl.ds(f * piece, piece), :], tiles[t + 1].reshape(slots, WIDE),
+                    rows = pl.ds(f * piece, piece)
+                    got = jnp.dot(hid_t[d, rows, :], tiles[s * CORES + h].reshape(slots, WIDE),
                                   preferred_element_type=F32)
-                    tiles[t, f] = got.astype(BF).reshape(SIDE, both, WIDE)
-
-        @pl.when(s == chunks)
-        def _():
-            await_bytes(hid_t.at[1], xh_sem)
+                    if prior:
+                        got = got + total[k * CORES + h, rows, :].astype(F32)
+                    total[k * CORES + h, rows, :] = got.astype(BF)
+
+        @pl.when(d == 0)
+        def _():
+            add_product(total, False)
 
         @pl.when(d == 1)
         def _():
-            @pl.loop(0, CORES)
-            def _(h):
-                t = s * CORES + h
-
-                @pl.when(s > chunks)
-                def _():
-                    await_bytes(done.at[h], done_sem.at[h])
-
-                @pl.loop(0, SIDE)
-                def _(f):
-                    got = jnp.dot(hid_t[1, pl.ds(f * piece, piece), :], tiles[t + 1].reshape(slots, WIDE),
-                                  preferred_element_type=F32)
-                    prior = tiles[t - chunks * CORES, f].reshape(piece, WIDE)
-                    done[h, pl.ds(f * piece, piece), :] = (got + prior.astype(F32)).astype(BF)
-
-                pltpu.make_async_copy(
-                    done.at[h],
-                    out_ref.at[:, pl.ds(pl.multiple_of(h * half + k * WIDE, LANES), WIDE)],
-                    done_sem.at[h]).start()
-
-    def transpose_hidden():
+            add_product(total, True)
+
+    def transpose_hidden(d):
         parts = slots // WIDE
-        for n in range(2 * parts):
+        for n in range((1 - d) * parts, (2 - d) * parts):
             load_hidden(n).wait()
             into = hid_out if n < parts else hid_t.at[0]
             part = n % parts
@@ -320,23 +308,23 @@
     stage_a(jnp.int32(0))
     send(own_tab, tab.at[1], xsend_sem.at[1], xt_sem, mirror)
     stage_a(jnp.int32(1))
+    stage_a(jnp.int32(2))
     stage_b(jnp.int32(0))
-    transpose_hidden()
+    transpose_hidden(1)
     send(hid_out, hid_t.at[1], xsend_sem.at[2], xh_sem, mirror)
+    stage_b(jnp.int32(1))
+    stage_c(jnp.int32(0))
+    transpose_hidden(0)
 
     def turn(i, carry):
-        for lag, work in ((0, stage_a), (1, stage_b), (2, stage_c), (3, stage_d), (4, stage_e)):
-            skip = {0: 2, 1: 1}.get(lag, 0)
-
+        for lag, skip, work in LAGS:
             @pl.when((i - lag >= skip) & (i - lag < steps))
             def _():
-                work(i - lag)
+                (stage_a, stage_b, stage_c, stage_d, stage_e)[work](i - lag)
         return carry
 
-    lax.fori_loop(2, steps + 4, turn, 0)
-
-    for h in range(CORES):
-        await_bytes(done.at[h], done_sem.at[h])
+    lax.fori_loop(3, steps + LAGS[-1][0], turn, 0)
+
     for track in range(TRACKS):
         await_bytes(to_far.at[track], far_send.at[track])
         await_bytes(to_sib.at[track], sib_send.at[track])
@@ -352,6 +340,21 @@
     for d in range(2):
         await_bytes(tabs.at[d, 0, pl.ds(0, 7)], tab_send.at[d])
         await_bytes(tabs.at[d, pl.ds(1, 2)], tab_pair_send.at[d])
+
+
+def finish(total, out_ref, sem):
+    count, units, wide = total.shape
+    chunks = count // CORES
+
+    def put(n):
+        k, h = n // CORES, n % CORES
+        cols = pl.ds(h * chunks * wide + k * wide, wide)
+        return pltpu.make_async_copy(total.at[n], out_ref.at[:, cols], sem.at[n])
+
+    for n in range(count):
+        put(n).start()
+    for n in range(count):
+        put(n).wait()
 
 
 def on_device(ranks, grad_rows, expert_ids, gate_buckets, saved_hidden):
@@ -365,39 +368,48 @@
     both = CORES * cap
     steps = width // WIDE
     dma = pltpu.SemaphoreType.DMA
-    result = pl.pallas_call(
+    (total,) = pl.pallas_call(
         functools.partial(kernel, ranks, cap),
-        out_shape=jax.ShapeDtypeStruct((units, width), BF),
+        out_shape=[
+            pltpu.VMEM((steps, units, WIDE), BF),
+        ],
         in_specs=[
             pl.BlockSpec(memory_space=pl.ANY),
             pl.BlockSpec(memory_space=pltpu.VMEM),
             pl.BlockSpec(memory_space=pltpu.VMEM),
             pl.BlockSpec(memory_space=pl.ANY),
         ],
-        out_specs=pl.BlockSpec(memory_space=pl.ANY),
+        out_specs=[pl.BlockSpec(memory_space=pltpu.VMEM)],
         scratch_shapes=[
             pltpu.VMEM((2, tokens, width), BF),
             pltpu.VMEM((steps, SIDE * CORES, tokens, WIDE), BF),
             pltpu.VMEM((steps, 2, SIDE * CORES, tokens, LANES), BF),
-            pltpu.VMEM((1 + steps * CORES, SIDE, SIDE, both, WIDE), BF),
+            pltpu.VMEM((steps * CORES, SIDE, SIDE, both, WIDE), BF),
             pltpu.VMEM((2, units, slots), BF),
             pltpu.VMEM((units, slots), BF),
             pltpu.VMEM((2, WIDE, units), BF),
             pltpu.VMEM((SIDE, 14 * both, CORES * tokens), BF),
-            pltpu.VMEM((3, top, tokens), F32),
-            pltpu.VMEM((2, 3, top, tokens), F32),
-            pltpu.VMEM((2, 3, SIDE * CORES, 3, top, tokens), F32),
+            pltpu.VMEM((2, top, tokens), F32),
+            pltpu.VMEM((2, 2, top, tokens), F32),
+            pltpu.VMEM((2, 3, SIDE * CORES, 2, top, tokens), F32),
             pltpu.VMEM((TRACKS, 2, CORES, 2, SIDE, both, LANES), BF),
             pltpu.VMEM((TRACKS, 2, 2, SIDE, both, LANES), BF),
-            pltpu.VMEM((CORES, units, WIDE), BF),
             dma, dma((steps // 2,)), dma, dma, dma((3,)), dma((2,)),
             dma((steps, 3)), dma((steps,)), dma((steps,)), dma((steps,)), dma((steps,)),
             dma((2, 3)), dma((2,)), dma((2,)), dma((2,)), dma((2,)),
-            dma((steps * CORES,)), dma((TRACKS,)), dma((TRACKS,)), dma((2,)),
+            dma((steps * CORES,)), dma((TRACKS,)), dma((TRACKS,)),
         ],
         compiler_params=pltpu.CompilerParams(
-            collective_id=0, has_side_effects=True, vmem_limit_bytes=66 * 1024 * 1000),
+            collective_id=0, has_side_effects=True, vmem_limit_bytes=VLIM),
     )(tok, ids, gates, hid)
+    result = pl.pallas_call(
+        finish,
+        out_shape=jax.ShapeDtypeStruct((units, width), BF),
+        in_specs=[pl.BlockSpec(memory_space=pltpu.VMEM)],
+        out_specs=pl.BlockSpec(memory_space=pl.ANY),
+        scratch_shapes=[dma((steps,))],
+        compiler_params=pltpu.CompilerParams(vmem_limit_bytes=4 * 1024 * 1024),
+    )(total)
     return result[None, None]
 
 

time: 157 us -> 145 us (0.924)
  local copies, waits for them, and re-layouts: 7.85 us -> 0 us
  Pallas kernels: 149 us -> 145 us
    unnamed x1 -> x0, local copies, waits for them, and re-layouts: 7.85 us -> none
    pallas_call x1 -> x2, Pallas kernels: 149 us -> 145 us  [the longest x1 141 us: on_device(): pl.pallas_call(functools.partial(kernel, ranks, cap), out_shape=[pltpu.VM...]
where the time goes in v3:
time: 145 us
  Pallas kernels  145 us (100%)
    pallas_call x1, Pallas kernels, on_device(): pl.pallas_call(functools.partial(kernel, ranks, cap), out_shape=[pltpu.VM...  141 us
    pallas_call x1, Pallas kernels, on_device(): pl.pallas_call(finish, out_shape=jax.ShapeDtypeStruct((units, width), BF)...  3.65 us

profile of v3, /device:TPU:1, one launch (start us, length us, event | category | flops | bytes accessed | tf_op | source)
XLA Modules:
  0.0 145.0 jit_solution(3094476152473442892)
XLA Ops:
  0.0 141.3 %shard_map.46.total = bf16[14,1280,256]{2,1,0:T(8,128)(2,1)S(1)} custom-call(bf16[2,128,3584]{2,1,0:T(8,128)(2,1)} %bitcast.10, s32[2,8,128]{2,1,0:T(8,128)} %bitcast.11, s32[2,8,128]{2,1,0:T(8,128)} %bitcast.12, bf16[2,1280,1280]{2,1,0:T(8,128)(2,1)} %bitcast.9), custom_call_target="tpu_custom_call" | custom-call | tf_op jit(solution)/shard_map/pallas_call | solution.py:371
  141.3 3.7 %shard_map.47 = bf16[1280,3584]{1,0:T(8,128)(2,1)} custom-call(bf16[14,1280,256]{2,1,0:T(8,128)(2,1)S(1)} %shard_map.46.total), custom_call_target="tpu_custom_call" | custom-call | tf_op jit(solution)/shard_map/pallas_call | solution.py:405

commit v4 on v3

--- a/solution.py
+++ b/solution.py
@@ -13,8 +13,9 @@
 LANES = 128
 WIDE = 2 * LANES
 TRACKS = 3
-LAGS = ((0, 3, 0), (1, 2, 1), (2, 1, 2), (4, 0, 3), (6, 0, 4))
-VLIM = 50 * 1024 * 1024
+AHEAD = 7
+LAGS = ((0, 7, 0), (5, 2, 1), (6, 1, 2), (8, 0, 3), (10, 0, 4))
+VLIM = 46 * 1024 * 1024
 BF = jnp.bfloat16
 F32 = jnp.float32
 
@@ -23,10 +24,10 @@
     return lax.rem(i + 2 * SIDE, SIDE)
 
 
-def kernel(ranks, cap, tok_ref, ids_ref, gate_ref, hid_ref, total,
-           src, ring, pair, tiles, hid_t, hid_out, stage, select, own_tab, tab, tabs,
+def kernel(ranks, cap, tok_ref, ids_ref, gate_ref, hid_ref, total, last, hid_two,
+           src, ring, pair, tiles, hid_one, hid_out, stage, select, own_tab, tab, tabs,
            to_far, to_sib,
-           src_sem, x_sem, xt_sem, xh_sem, xsend_sem, stage_sem,
+           x_sem, xt_sem, xh_sem, xsend_sem, stage_sem,
            ring_sem, own_sem, ring_send, pair_sem, pair_send,
            tab_sem, tab_own_sem, tab_send, tab_pair_sem, tab_pair_send,
            tile_sem, far_send, sib_send):
@@ -69,9 +70,6 @@
     def await_bytes(ref, sem):
         pltpu.make_async_copy(ref, ref, sem).wait()
 
-    first = pltpu.make_async_copy(tok_ref.at[0], src.at[0], src_sem)
-    first.start()
-
     def load_hidden(n):
         d, part = (1, n) if n < slots // WIDE else (0, n - slots // WIDE)
         return pltpu.make_async_copy(
@@ -88,12 +86,6 @@
             friends.append(at(z, wrap(y + turn), core))
     for friend in friends:
         pl.semaphore_signal(barrier, inc=1, device_id=friend, device_id_type=MESH)
-    pl.semaphore_wait(barrier, len(friends))
-
-    for k in range(chunks):
-        for h in range(CORES):
-            cols = pl.ds(h * half + k * WIDE, WIDE)
-            send(tok_ref.at[1, :, cols], src.at[1, :, cols], xsend_sem.at[0], x_sem.at[k], mirror)
 
     e_row = lax.broadcasted_iota(jnp.int32, (SIDE * SIDE * CORES, tokens), 0)
     before = (lax.broadcasted_iota(jnp.int32, (tokens, tokens), 0)
@@ -111,7 +103,7 @@
         into[0] = ids.astype(F32) * cap + jnp.concatenate(spots, axis=0)
         into[1] = gate_ref[d].astype(F32) / 64.0
 
-    first.wait()
+    pl.semaphore_wait(barrier, len(friends))
 
     def ring_out(source, dest, sems, send_sem, own, cols_of):
         for h in range(CORES):
@@ -133,22 +125,28 @@
     def step_cols(k):
         return lambda ref, h: ref.at[:, pl.ds(pl.multiple_of(h * half + k * WIDE, LANES), WIDE)]
 
+    def tables_out(d):
+        ring_out(tab.at[d], tabs.at[d, 0], tab_sem.at[d], tab_send.at[d], tab_own_sem.at[d], lambda ref, h: ref)
+
+    def rows_out(s, source, k):
+        ring_out(source, ring.at[s], ring_sem.at[s], ring_send.at[s], own_sem.at[s], step_cols(k))
+
     def stage_a(s):
-        d, k = s // chunks, lax.rem(s, chunks)
-
-        @pl.when(d == 1)
-        def _():
-            await_bytes(src.at[1, :, pl.ds(0, 2 * WIDE)], x_sem.at[k])
+        k = s - chunks
+
+        @pl.when(k < 0)
+        def _():
+            rows_out(s, tok_ref.at[0], s)
 
         @pl.when(k == 0)
         def _():
-            @pl.when(d == 1)
-            def _():
-                await_bytes(tab.at[1], xt_sem)
-            ring_out(tab.at[d], tabs.at[d, 0], tab_sem.at[d], tab_send.at[d], tab_own_sem.at[d],
-                     lambda ref, h: ref)
-
-        ring_out(src.at[d], ring.at[s], ring_sem.at[s], ring_send.at[s], own_sem.at[s], step_cols(k))
+            await_bytes(tab.at[1], xt_sem)
+            tables_out(1)
+
+        @pl.when(k >= 0)
+        def _():
+            await_bytes(src.at[:, pl.ds(0, 2 * WIDE)], x_sem.at[k])
+            rows_out(s, src, k)
 
     def stage_b(s):
         d, k = s // chunks, lax.rem(s, chunks)
@@ -239,44 +237,55 @@
                     own_at = 0 if p == 0 else 2 * both
                     far_at = 2 * both if p == 0 else 0
                     z_, y_ = (1 - c) * a_ + c * b_, (1 - c) * b_ + c * a_
-                    tiles[s * CORES + c, z_, y_, :, p * LANES:(p + 1) * LANES] = got[own_at:own_at + both]
+                    kept = got[own_at:own_at + both]
+
+                    @pl.when(s < steps - 1)
+                    def _():
+                        tiles[s * CORES + c, z_, y_, :, p * LANES:(p + 1) * LANES] = kept
+
+                    @pl.when(s == steps - 1)
+                    def _():
+                        last[c, z_, y_, :, p * LANES:(p + 1) * LANES] = kept
+
                     to_sib[track, p, b_at, a_] = got[own_at + both:own_at + 2 * both]
                     for core in range(CORES):
                         to_far[track, p, core, b_at, a_] = got[far_at + core * both:far_at + (core + 1) * both]
 
-        for h in range(CORES):
-            @pl.when(c == h)
-            def _():
-                into = tiles.at[s * CORES + h]
-                for p in range(2):
-                    cols = pl.ds(p * LANES, LANES)
-                    friend = near if p == 0 else far
-                    other = far if p == 0 else near
-                    for b_at in range(2):
-                        b_ = mine_b if b_at == 0 else friend
-                        part = into.at[:, b_, :, cols] if h == 0 else into.at[b_, :, :, cols]
-                        for core in range(CORES):
-                            send(to_far.at[track, p, core, b_at], part, far_send.at[track],
-                                 tile_sem.at[s * CORES + h], at_ab(mine_a, other, core))
-                        send(to_sib.at[track, p, b_at], part, sib_send.at[track],
-                             tile_sem.at[s * CORES + h], sibling)
+        for final_step, goal in ((s < steps - 1, lambda h: tiles.at[s * CORES + h]),
+                                 (s == steps - 1, lambda h: last.at[h])):
+            for h in range(CORES):
+                @pl.when((c == h) & final_step)
+                def _():
+                    into = goal(h)
+                    for p in range(2):
+                        cols = pl.ds(p * LANES, LANES)
+                        friend = near if p == 0 else far
+                        other = far if p == 0 else near
+                        for b_at in range(2):
+                            b_ = mine_b if b_at == 0 else friend
+                            part = into.at[:, b_, :, cols] if h == 0 else into.at[b_, :, :, cols]
+                            for core in range(CORES):
+                                send(to_far.at[track, p, core, b_at], part, far_send.at[track],
+                                     tile_sem.at[s * CORES + h], at_ab(mine_a, other, core))
+                            send(to_sib.at[track, p, b_at], part, sib_send.at[track],
+                                 tile_sem.at[s * CORES + h], sibling)
 
     def stage_e(s):
         d, k = s // chunks, lax.rem(s, chunks)
-        await_bytes(tiles.at[0, pl.ds(0, 2)], tile_sem.at[s * CORES + c])
+        await_bytes(tiles.at[0, pl.ds(0, SIDE // 2)], tile_sem.at[s * CORES + c])
         await_bytes(tiles.at[0], tile_sem.at[s * CORES + 1 - c])
 
         @pl.when(s == chunks)
         def _():
-            await_bytes(hid_t.at[1], xh_sem)
-
-        def add_product(dest, prior):
+            await_bytes(hid_two, xh_sem)
+
+        def add_product(hid, prior):
             @pl.loop(0, CORES)
             def _(h):
                 @pl.loop(0, SIDE)
                 def _(f):
                     rows = pl.ds(f * piece, piece)
-                    got = jnp.dot(hid_t[d, rows, :], tiles[s * CORES + h].reshape(slots, WIDE),
+                    got = jnp.dot(hid[rows, :], tiles[s * CORES + h].reshape(slots, WIDE),
                                   preferred_element_type=F32)
                     if prior:
                         got = got + total[k * CORES + h, rows, :].astype(F32)
@@ -284,17 +293,17 @@
 
         @pl.when(d == 0)
         def _():
-            add_product(total, False)
-
-        @pl.when(d == 1)
-        def _():
-            add_product(total, True)
+            add_product(hid_one, False)
+
+        @pl.when((d == 1) & (s < steps - 1))
+        def _():
+            add_product(hid_two, True)
 
     def transpose_hidden(d):
         parts = slots // WIDE
         for n in range((1 - d) * parts, (2 - d) * parts):
             load_hidden(n).wait()
-            into = hid_out if n < parts else hid_t.at[0]
+            into = hid_out if n < parts else hid_one
             part = n % parts
 
             @pl.loop(0, units // WIDE)
@@ -305,13 +314,18 @@
             if n + 2 < 2 * parts:
                 load_hidden(n + 2).start()
 
-    stage_a(jnp.int32(0))
-    send(own_tab, tab.at[1], xsend_sem.at[1], xt_sem, mirror)
-    stage_a(jnp.int32(1))
-    stage_a(jnp.int32(2))
+    for s in range(AHEAD):
+        rows_out(s, tok_ref.at[0], s)
+        if s == 0:
+            tables_out(0)
+            send(own_tab, tab.at[1], xsend_sem.at[1], xt_sem, mirror)
+    for k in range(chunks):
+        for h in range(CORES):
+            cols = pl.ds(h * half + k * WIDE, WIDE)
+            send(tok_ref.at[1, :, cols], src.at[:, cols], xsend_sem.at[0], x_sem.at[k], mirror)
     stage_b(jnp.int32(0))
     transpose_hidden(1)
-    send(hid_out, hid_t.at[1], xsend_sem.at[2], xh_sem, mirror)
+    send(hid_out, hid_two, xsend_sem.at[2], xh_sem, mirror)
     stage_b(jnp.int32(1))
     stage_c(jnp.int32(0))
     transpose_hidden(0)
@@ -323,12 +337,12 @@
                 (stage_a, stage_b, stage_c, stage_d, stage_e)[work](i - lag)
         return carry
 
-    lax.fori_loop(3, steps + LAGS[-1][0], turn, 0)
+    lax.fori_loop(AHEAD, steps + LAGS[-1][0], turn, 0)
 
     for track in range(TRACKS):
         await_bytes(to_far.at[track], far_send.at[track])
         await_bytes(to_sib.at[track], sib_send.at[track])
-    await_bytes(src.at[1], xsend_sem.at[0])
+    await_bytes(src, xsend_sem.at[0])
     await_bytes(own_tab, xsend_sem.at[1])
     await_bytes(hid_out, xsend_sem.at[2])
 
@@ -342,19 +356,30 @@
         await_bytes(tabs.at[d, pl.ds(1, 2)], tab_pair_send.at[d])
 
 
-def finish(total, out_ref, sem):
+def finish(total, last, hid_two, out_ref, made, sem):
     count, units, wide = total.shape
+    slots = hid_two.shape[1]
     chunks = count // CORES
-
-    def put(n):
-        k, h = n // CORES, n % CORES
+    piece = units // SIDE
+
+    def put(k, h):
         cols = pl.ds(h * chunks * wide + k * wide, wide)
-        return pltpu.make_async_copy(total.at[n], out_ref.at[:, cols], sem.at[n])
-
-    for n in range(count):
-        put(n).start()
-    for n in range(count):
-        put(n).wait()
+        rows = total.at[k * CORES + h] if k < chunks - 1 else made.at[h]
+        return pltpu.make_async_copy(rows, out_ref.at[:, cols], sem.at[k * CORES + h])
+
+    for k in range(chunks - 1):
+        for h in range(CORES):
+            put(k, h).start()
+    for h in range(CORES):
+        @pl.loop(0, SIDE)
+        def _(f):
+            rows = pl.ds(f * piece, piece)
+            got = jnp.dot(hid_two[rows, :], last[h].reshape(slots, wide), preferred_element_type=F32)
+            made[h, rows, :] = (got + total[count - CORES + h, rows, :].astype(F32)).astype(BF)
+        put(chunks - 1, h).start()
+    for k in range(chunks):
+        for h in range(CORES):
+            put(k, h).wait()
 
 
 def on_device(ranks, grad_rows, expert_ids, gate_buckets, saved_hidden):
@@ -368,10 +393,12 @@
     both = CORES * cap
     steps = width // WIDE
     dma = pltpu.SemaphoreType.DMA
-    (total,) = pl.pallas_call(
+    total, last, hid_two = pl.pallas_call(
         functools.partial(kernel, ranks, cap),
         out_shape=[
             pltpu.VMEM((steps, units, WIDE), BF),
+            pltpu.VMEM((CORES, SIDE, SIDE, both, WIDE), BF),
+            pltpu.VMEM((units, slots), BF),
         ],
         in_specs=[
             pl.BlockSpec(memory_space=pl.ANY),
@@ -379,13 +406,13 @@
             pl.BlockSpec(memory_space=pltpu.VMEM),
             pl.BlockSpec(memory_space=pl.ANY),
         ],
-        out_specs=[pl.BlockSpec(memory_space=pltpu.VMEM)],
+        out_specs=[pl.BlockSpec(memory_space=pltpu.VMEM)] * 3,
         scratch_shapes=[
-            pltpu.VMEM((2, tokens, width), BF),
+            pltpu.VMEM((tokens, width), BF),
             pltpu.VMEM((steps, SIDE * CORES, tokens, WIDE), BF),
             pltpu.VMEM((steps, 2, SIDE * CORES, tokens, LANES), BF),
-            pltpu.VMEM((steps * CORES, SIDE, SIDE, both, WIDE), BF),
-            pltpu.VMEM((2, units, slots), BF),
+            pltpu.VMEM(((steps - 1) * CORES, SIDE, SIDE, both, WIDE), BF),
+            pltpu.VMEM((units, slots), BF),
             pltpu.VMEM((units, slots), BF),
             pltpu.VMEM((2, WIDE, units), BF),
             pltpu.VMEM((SIDE, 14 * both, CORES * tokens), BF),
@@ -394,7 +421,7 @@
             pltpu.VMEM((2, 3, SIDE * CORES, 2, top, tokens), F32),
             pltpu.VMEM((TRACKS, 2, CORES, 2, SIDE, both, LANES), BF),
             pltpu.VMEM((TRACKS, 2, 2, SIDE, both, LANES), BF),
-            dma, dma((steps // 2,)), dma, dma, dma((3,)), dma((2,)),
+            dma((steps // 2,)), dma, dma, dma((3,)), dma((2,)),
             dma((steps, 3)), dma((steps,)), dma((steps,)), dma((steps,)), dma((steps,)),
             dma((2, 3)), dma((2,)), dma((2,)), dma((2,)), dma((2,)),
             dma((steps * CORES,)), dma((TRACKS,)), dma((TRACKS,)),
@@ -405,11 +432,11 @@
     result = pl.pallas_call(
         finish,
         out_shape=jax.ShapeDtypeStruct((units, width), BF),
-        in_specs=[pl.BlockSpec(memory_space=pltpu.VMEM)],
+        in_specs=[pl.BlockSpec(memory_space=pltpu.VMEM)] * 3,
         out_specs=pl.BlockSpec(memory_space=pl.ANY),
-        scratch_shapes=[dma((steps,))],
+        scratch_shapes=[pltpu.VMEM((CORES, units, WIDE), BF), dma((steps,))],
         compiler_params=pltpu.CompilerParams(vmem_limit_bytes=4 * 1024 * 1024),
-    )(total)
+    )(total, last, hid_two)
     return result[None, None]
 
 

time: 145 us -> 140 us (0.966)
  Pallas kernels: 145 us -> 140 us
    pallas_call x1, Pallas kernels: 141 us -> 136 us  [on_device(): pl.pallas_call(functools.partial(kernel, ranks, cap), out_shape=[pltpu.VM...]
where the time goes in v4:
time: 140 us
  Pallas kernels  140 us (100%)
    pallas_call x1, Pallas kernels, on_device(): pl.pallas_call(functools.partial(kernel, ranks, cap), out_shape=[pltpu.VM...  136 us
    pallas_call x1, Pallas kernels, on_device(): pl.pallas_call(finish, out_shape=jax.ShapeDtypeStruct((units, width), BF)...  4.08 us

profile of v4, /device:TPU:1, one launch (start us, length us, event | category | flops | bytes accessed | tf_op | source)
XLA Modules:
  0.0 140.1 jit_solution(2025326220932278270)
XLA Ops:
  0.0 136.1 %shard_map.46 = (bf16[14,1280,256]{2,1,0:T(8,128)(2,1)S(1)}, bf16[2,4,4,80,256]{4,3,2,1,0:T(8,128)(2,1)S(1)}, bf16[1280,1280]{1,0:T(8,128)(2,1)S(1)}) custom-call(bf16[2,128,3584]{2,1,0:T(8,128)(2,1)} %bitcast.10, s32[2,8,128]{2,1,0:T(8,128)} %bitcast.11, s32[2,8,128]{2,1,0:T(8,128)} %bitcast.12, bf16[2,1280,1280]{2,1,0:T(8,128)(2,1)} %bitcast.9), custom_call_target="tpu_custom_call" | custom-call | tf_op jit(solution)/shard_map/pallas_call | solution.py:396
  136.1 4.1 %shard_map.47 = bf16[1280,3584]{1,0:T(8,128)(2,1)} custom-call(bf16[14,1280,256]{2,1,0:T(8,128)(2,1)S(1)} %get-tuple-element.8.total, bf16[2,4,4,80,256]{4,3,2,1,0:T(8,128)(2,1)S(1)} %get-tuple-element.9.last, bf16[1280,1280]{1,0:T(8,128)(2,1)S(1)} %get-tuple-element.10.hid_two), custom_call_target="tpu_custom_call" | custom-call | tf_op jit(solution)/shard_map/pallas_call | solution.py:432

commit v5 on v4

--- a/solution.py
+++ b/solution.py
@@ -14,8 +14,11 @@
 WIDE = 2 * LANES
 TRACKS = 3
 AHEAD = 7
-LAGS = ((0, 7, 0), (5, 2, 1), (6, 1, 2), (8, 0, 3), (10, 0, 4))
+LAGS = ((0, 7, 0), (5, 2, 1), (6, 1, 2), (7, 0, 3), (9, 0, 4))
 VLIM = 46 * 1024 * 1024
+INNER = ((0, 0), (0, -1), (-1, -1), (1, 0), (1, 1), (2, 1))
+LEAVES = (((0, 1), (-1, 0)), ((0, -1), (1, 0)), ((-1, 0), (0, -1)), ((1, 0),), ((0, 1),), ((0, 1), (1, 0)))
+SIGNS = (1, -1)
 BF = jnp.bfloat16
 F32 = jnp.float32
 
@@ -25,11 +28,11 @@
 
 
 def kernel(ranks, cap, tok_ref, ids_ref, gate_ref, hid_ref, total, last, hid_two,
-           src, ring, pair, tiles, hid_one, hid_out, stage, select, own_tab, tab, tabs,
+           src, full, tiles, hid_one, hid_out, stage, select, own_tab, tab, tabs,
            to_far, to_sib,
            x_sem, xt_sem, xh_sem, xsend_sem, stage_sem,
-           ring_sem, own_sem, ring_send, pair_sem, pair_send,
-           tab_sem, tab_own_sem, tab_send, tab_pair_sem, tab_pair_send,
+           own_sem, sib_sem, hop_sem, hop_send,
+           tab_own_sem, tab_sib_sem, tab_hop_sem, tab_hop_send,
            tile_sem, far_send, sib_send):
     tokens, width = tok_ref.shape[1], tok_ref.shape[2]
     slots, units = hid_ref.shape[1], hid_ref.shape[2]
@@ -46,10 +49,6 @@
     z = expert // (CORES * SIDE)
     mine_a = (1 - c) * z + c * y
     mine_b = (1 - c) * y + c * z
-    step_a = lax.rem(mine_b, 2)
-    near = wrap(mine_b + 1 - 2 * step_a)
-    far = wrap(mine_b - 1 + 2 * step_a)
-
     def at(z_, y_, core):
         return {"pipe": rank, "expert": (z_ * SIDE + y_) * CORES + core}
 
@@ -105,31 +104,31 @@
 
     pl.semaphore_wait(barrier, len(friends))
 
-    def ring_out(source, dest, sems, send_sem, own, cols_of):
-        for h in range(CORES):
-            a_h = z if h == 0 else y
-            for turn in (1, -1):
-                dev = at(wrap(z + turn), y, 0) if h == 0 else at(z, wrap(y + turn), 1)
-                which = 2 * c if turn == 1 else 2 - c
-                send(cols_of(source, h), dest.at[a_h * CORES + c], send_sem, sems.at[which], dev)
-        sib_a = c * z + (1 - c) * y
-        send(cols_of(source, 1 - c), dest.at[sib_a * CORES + c], send_sem, sems.at[2], sibling)
-        pltpu.make_async_copy(cols_of(source, c), dest.at[mine_a * CORES + c], own).start()
-
-    def ring_on(dest, sems, send_sem):
-        for turn, core in ((1, 0), (-1, 1)):
-            part = dest.at[wrap(mine_a - turn) * CORES + core]
-            await_bytes(part, sems.at[core])
-            send(part, part, send_sem, sems.at[2], at_ab(wrap(mine_a + turn), mine_b, c))
-
-    def step_cols(k):
-        return lambda ref, h: ref.at[:, pl.ds(pl.multiple_of(h * half + k * WIDE, LANES), WIDE)]
+    def first_hop(sources, dest, own, sib, sem, send_sem):
+        for p, sign in enumerate(SIGNS):
+            for h in range(CORES):
+                for n in (1, 3):
+                    da, db = sign * INNER[n][0], sign * INNER[n][1]
+                    dev = at(wrap(z + da), wrap(y + db), 0) if h == 0 else at(wrap(z + db), wrap(y + da), 1)
+                    send(sources(h, p), dest.at[p, n, c], send_sem, sem, dev)
+            send(sources(1 - c, p), dest.at[p, 0, c], send_sem, sib, sibling)
+            pltpu.make_async_copy(sources(c, p), dest.at[p, 0, c], own).start()
+
+    def next_hop(dest, sem, send_sem, pairs):
+        for p, sign in enumerate(SIGNS):
+            for n, m in pairs:
+                da, db = (sign * (INNER[m][i] - INNER[n][i]) for i in range(2))
+                send(dest.at[p, n], dest.at[p, m], send_sem, sem,
+                     at_ab(wrap(mine_a + da), wrap(mine_b + db), c))
 
     def tables_out(d):
-        ring_out(tab.at[d], tabs.at[d, 0], tab_sem.at[d], tab_send.at[d], tab_own_sem.at[d], lambda ref, h: ref)
+        first_hop(lambda h, p: tab.at[d], tabs.at[d], tab_own_sem.at[d], tab_sib_sem.at[d],
+                  tab_hop_sem.at[d, 0], tab_hop_send.at[d, 0])
 
     def rows_out(s, source, k):
-        ring_out(source, ring.at[s], ring_sem.at[s], ring_send.at[s], own_sem.at[s], step_cols(k))
+        def part(h, p):
+            return source.at[:, pl.ds(pl.multiple_of(h * half + k * WIDE + p * LANES, LANES), LANES)]
+        first_hop(part, full.at[s], own_sem.at[s], sib_sem.at[s], hop_sem.at[s, 0], hop_send.at[s, 0])
 
     def stage_a(s):
         k = s - chunks
@@ -153,35 +152,31 @@
 
         @pl.when(k == 0)
         def _():
-            ring_on(tabs.at[d, 0], tab_sem.at[d], tab_send.at[d])
-
-        ring_on(ring.at[s], ring_sem.at[s], ring_send.at[s])
+            await_bytes(tabs.at[d, 0, pl.ds(0, 4)], tab_hop_sem.at[d, 0])
+            next_hop(tabs.at[d], tab_hop_sem.at[d, 1], tab_hop_send.at[d, 1], ((1, 2), (3, 4)))
+
+        await_bytes(full.at[s, 0, pl.ds(0, 4)], hop_sem.at[s, 0])
+        next_hop(full.at[s], hop_sem.at[s, 1], hop_send.at[s, 1], ((1, 2), (3, 4)))
 
     def stage_c(s):
         d, k = s // chunks, lax.rem(s, chunks)
 
         @pl.when(k == 0)
         def _():
-            await_bytes(tabs.at[d, 0, pl.ds(0, 5)], tab_sem.at[d, 2])
-            await_bytes(tabs.at[d, 0, 0], tab_own_sem.at[d])
-            for p, friend in ((0, near), (1, far)):
-                send(tabs.at[d, 0], tabs.at[d, 1 + p], tab_pair_send.at[d], tab_pair_sem.at[d],
-                     at_ab(mine_a, friend, c))
-
-        await_bytes(ring.at[s, pl.ds(0, 5)], ring_sem.at[s, 2])
-        await_bytes(ring.at[s, 0], own_sem.at[s])
-        for p, friend in ((0, near), (1, far)):
-            send(ring.at[s, :, :, pl.ds(p * LANES, LANES)], pair.at[s, p], pair_send.at[s],
-                 pair_sem.at[s], at_ab(mine_a, friend, c))
+            await_bytes(tabs.at[d, 0, pl.ds(0, 4)], tab_hop_sem.at[d, 1])
+            next_hop(tabs.at[d], tab_hop_sem.at[d, 2], tab_hop_send.at[d, 2], ((4, 5),))
+
+        await_bytes(full.at[s, 0, pl.ds(0, 4)], hop_sem.at[s, 1])
+        next_hop(full.at[s], hop_sem.at[s, 2], hop_send.at[s, 2], ((4, 5),))
 
     row = lax.broadcasted_iota(jnp.int32, (both, CORES * tokens), 0)
     lane = lax.broadcasted_iota(jnp.int32, (both, CORES * tokens), 1)
     target = jnp.where((row < cap) == (lane < tokens), jnp.where(row < cap, row, row - cap), -2).astype(F32)
 
-    def select_rows(d, where_, a_, e):
+    def select_rows(d, p, n, e):
         found = []
         for core in range(CORES):
-            t = tabs.at[d, where_, a_ * CORES + core]
+            t = tabs.at[d, p, n, core]
             local = t[0] - (e * cap).astype(F32)
             hit = (local >= 0.0) & (local < cap)
             spot = jnp.sum(jnp.where(hit, local + 1.0, 0.0), axis=0, keepdims=True) - 1.0
@@ -191,18 +186,23 @@
         weight = jnp.concatenate([f[1] for f in found], axis=1)
         return jnp.where(spot == target, weight, 0.0).astype(BF)
 
-    own2 = [(mine_b, c), (mine_b, 1 - c)]
-    near2 = [(near, 0), (near, 1)]
-    far2 = [(far, 0), (far, 1)]
-    plan = [(0, x) for x in near2 + own2 + far2] + [(1, x) for x in own2 + far2] + [(2, x) for x in near2 + own2]
+    blocks, start = [], {}
+    for p, sign in enumerate(SIGNS):
+        for n in range(len(INNER)):
+            start[(p, n)] = len(blocks)
+            blocks += [(p, n, mine_a, mine_b, c), (p, n, mine_a, mine_b, 1 - c)]
+            for da, db in LEAVES[n]:
+                blocks += [(p, n, wrap(mine_a + sign * da), wrap(mine_b + sign * db), core) for core in range(CORES)]
 
     def build_select(d):
-        @pl.loop(0, SIDE)
-        def _(a_):
-            for n, (where_, (b_, core)) in enumerate(plan):
-                select[a_, pl.ds(n * both, both), :] = select_rows(d, where_, a_, expert_ab(mine_a, b_, core))
-
-    lead = {(0, 0): 2, (0, 1): 6, (1, 0): 0, (1, 1): 10}
+        for i, (p, n, a_, b_, core) in enumerate(blocks):
+            select[i * both:(i + 1) * both, :] = select_rows(d, p, n, expert_ab(a_, b_, core))
+
+    def origin(p, n):
+        a_, b_ = (wrap(at_ - SIGNS[p] * off) for at_, off in zip((mine_a, mine_b), INNER[n]))
+        return (1 - c) * a_ + c * b_, (1 - c) * b_ + c * a_
+
+    first_leaf = [sum(len(LEAVES[m]) for m in range(n)) for n in range(len(INNER))]
 
     def stage_d(s):
         d, k = s // chunks, lax.rem(s, chunks)
@@ -210,7 +210,9 @@
 
         @pl.when(k == 0)
         def _():
-            await_bytes(tabs.at[d, pl.ds(1, 2)], tab_pair_sem.at[d])
+            await_bytes(tabs.at[d, 0, pl.ds(0, 2)], tab_hop_sem.at[d, 2])
+            await_bytes(tabs.at[d, 0, 0], tab_sib_sem.at[d])
+            await_bytes(tabs.at[d, 0, 0], tab_own_sem.at[d])
             build_select(d)
 
         @pl.when(s >= TRACKS)
@@ -218,61 +220,54 @@
             await_bytes(to_far.at[track], far_send.at[track])
             await_bytes(to_sib.at[track], sib_send.at[track])
 
-        await_bytes(ring.at[s], pair_sem.at[s])
+        await_bytes(full.at[s, 0, pl.ds(0, 2)], hop_sem.at[s, 2])
+        await_bytes(full.at[s, 0, 0], sib_sem.at[s])
+        await_bytes(full.at[s, 0, 0], own_sem.at[s])
         for p in range(2):
-            friend = near if p == 0 else far
-            for b_at in range(2):
-                b_ = mine_b if b_at == 0 else friend
-                start = lead[(p, b_at)] * both
-
-                @pl.loop(0, SIDE)
-                def _(a_):
-                    if b_at == 0:
-                        rows = ring[s, pl.ds(a_ * CORES, CORES), :, p * LANES:(p + 1) * LANES]
-                    else:
-                        rows = pair[s, p, pl.ds(a_ * CORES, CORES)]
-                    rows = rows.reshape(CORES * tokens, LANES)
-                    got = jnp.dot(select[a_, pl.ds(start, 4 * both), :], rows,
-                                  preferred_element_type=F32).astype(BF)
-                    own_at = 0 if p == 0 else 2 * both
-                    far_at = 2 * both if p == 0 else 0
-                    z_, y_ = (1 - c) * a_ + c * b_, (1 - c) * b_ + c * a_
-                    kept = got[own_at:own_at + both]
-
-                    @pl.when(s < steps - 1)
-                    def _():
-                        tiles[s * CORES + c, z_, y_, :, p * LANES:(p + 1) * LANES] = kept
-
-                    @pl.when(s == steps - 1)
-                    def _():
-                        last[c, z_, y_, :, p * LANES:(p + 1) * LANES] = kept
-
-                    to_sib[track, p, b_at, a_] = got[own_at + both:own_at + 2 * both]
+            for n in range(len(INNER)):
+                rows = full[s, p, n].reshape(CORES * tokens, LANES)
+                count = 2 + CORES * len(LEAVES[n])
+                got = jnp.dot(select[start[(p, n)] * both:(start[(p, n)] + count) * both, :], rows,
+                              preferred_element_type=F32).astype(BF)
+                z_, y_ = origin(p, n)
+
+                @pl.when(s < steps - 1)
+                def _():
+                    tiles[s * CORES + c, z_, y_, :, p * LANES:(p + 1) * LANES] = got[:both]
+
+                @pl.when(s == steps - 1)
+                def _():
+                    last[c, z_, y_, :, p * LANES:(p + 1) * LANES] = got[:both]
+
+                to_sib[track, p, n] = got[both:2 * both]
+                for i in range(len(LEAVES[n])):
                     for core in range(CORES):
-                        to_far[track, p, core, b_at, a_] = got[far_at + core * both:far_at + (core + 1) * both]
-
-        for final_step, goal in ((s < steps - 1, lambda h: tiles.at[s * CORES + h]),
-                                 (s == steps - 1, lambda h: last.at[h])):
-            for h in range(CORES):
-                @pl.when((c == h) & final_step)
-                def _():
-                    into = goal(h)
-                    for p in range(2):
-                        cols = pl.ds(p * LANES, LANES)
-                        friend = near if p == 0 else far
-                        other = far if p == 0 else near
-                        for b_at in range(2):
-                            b_ = mine_b if b_at == 0 else friend
-                            part = into.at[:, b_, :, cols] if h == 0 else into.at[b_, :, :, cols]
-                            for core in range(CORES):
-                                send(to_far.at[track, p, core, b_at], part, far_send.at[track],
-                                     tile_sem.at[s * CORES + h], at_ab(mine_a, other, core))
-                            send(to_sib.at[track, p, b_at], part, sib_send.at[track],
-                                 tile_sem.at[s * CORES + h], sibling)
+                        at_ = (2 + CORES * i + core) * both
+                        to_far[track, p, first_leaf[n] + i, core] = got[at_:at_ + both]
+
+        def hand_on(into):
+            for p, sign in enumerate(SIGNS):
+                for n in range(len(INNER)):
+                    z_, y_ = origin(p, n)
+                    part = into.at[z_, y_, :, pl.ds(p * LANES, LANES)]
+                    for i, (da, db) in enumerate(LEAVES[n]):
+                        for core in range(CORES):
+                            send(to_far.at[track, p, first_leaf[n] + i, core], part, far_send.at[track],
+                                 tile_sem.at[s * CORES + c],
+                                 at_ab(wrap(mine_a + sign * da), wrap(mine_b + sign * db), core))
+                    send(to_sib.at[track, p, n], part, sib_send.at[track], tile_sem.at[s * CORES + c], sibling)
+
+        @pl.when(s < steps - 1)
+        def _():
+            hand_on(tiles.at[s * CORES + c])
+
+        @pl.when(s == steps - 1)
+        def _():
+            hand_on(last.at[c])
 
     def stage_e(s):
         d, k = s // chunks, lax.rem(s, chunks)
-        await_bytes(tiles.at[0, pl.ds(0, SIDE // 2)], tile_sem.at[s * CORES + c])
+        await_bytes(to_far.at[0, 0], tile_sem.at[s * CORES + c])
         await_bytes(tiles.at[0], tile_sem.at[s * CORES + 1 - c])
 
         @pl.when(s == chunks)
@@ -282,9 +277,9 @@
         def add_product(hid, prior):
             @pl.loop(0, CORES)
             def _(h):
-                @pl.loop(0, SIDE)
+                @pl.loop(0, 1)
                 def _(f):
-                    rows = pl.ds(f * piece, piece)
+                    rows = pl.ds(f * (units // 1), units // 1)
                     got = jnp.dot(hid[rows, :], tiles[s * CORES + h].reshape(slots, WIDE),
                                   preferred_element_type=F32)
                     if prior:
@@ -348,12 +343,12 @@
 
     @pl.loop(0, steps)
     def _(s):
-        await_bytes(ring.at[s, pl.ds(0, 7)], ring_send.at[s])
-        await_bytes(ring.at[s], pair_send.at[s])
+        for hop, count in enumerate((5, 4, 2)):
+            await_bytes(full.at[s, 0, pl.ds(0, count)], hop_send.at[s, hop])
 
     for d in range(2):
-        await_bytes(tabs.at[d, 0, pl.ds(0, 7)], tab_send.at[d])
-        await_bytes(tabs.at[d, pl.ds(1, 2)], tab_pair_send.at[d])
+        for hop, count in enumerate((5, 4, 2)):
+            await_bytes(tabs.at[d, 0, pl.ds(0, count)], tab_hop_send.at[d, hop])
 
 
 def finish(total, last, hid_two, out_ref, made, sem):
@@ -409,21 +404,20 @@
         out_specs=[pl.BlockSpec(memory_space=pltpu.VMEM)] * 3,
         scratch_shapes=[
             pltpu.VMEM((tokens, width), BF),
-            pltpu.VMEM((steps, SIDE * CORES, tokens, WIDE), BF),
-            pltpu.VMEM((steps, 2, SIDE * CORES, tokens, LANES), BF),
+            pltpu.VMEM((steps, 2, len(INNER), CORES, tokens, LANES), BF),
             pltpu.VMEM(((steps - 1) * CORES, SIDE, SIDE, both, WIDE), BF),
             pltpu.VMEM((units, slots), BF),
             pltpu.VMEM((units, slots), BF),
             pltpu.VMEM((2, WIDE, units), BF),
-            pltpu.VMEM((SIDE, 14 * both, CORES * tokens), BF),
+            pltpu.VMEM((64 * both, CORES * tokens), BF),
             pltpu.VMEM((2, top, tokens), F32),
             pltpu.VMEM((2, 2, top, tokens), F32),
-            pltpu.VMEM((2, 3, SIDE * CORES, 2, top, tokens), F32),
-            pltpu.VMEM((TRACKS, 2, CORES, 2, SIDE, both, LANES), BF),
-            pltpu.VMEM((TRACKS, 2, 2, SIDE, both, LANES), BF),
+            pltpu.VMEM((2, 2, len(INNER), CORES, 2, top, tokens), F32),
+            pltpu.VMEM((TRACKS, 2, 10, CORES, both, LANES), BF),
+            pltpu.VMEM((TRACKS, 2, len(INNER), both, LANES), BF),
             dma((steps // 2,)), dma, dma, dma((3,)), dma((2,)),
-            dma((steps, 3)), dma((steps,)), dma((steps,)), dma((steps,)), dma((steps,)),
-            dma((2, 3)), dma((2,)), dma((2,)), dma((2,)), dma((2,)),
+            dma((steps,)), dma((steps,)), dma((steps, 3)), dma((steps, 3)),
+            dma((2,)), dma((2,)), dma((2, 3)), dma((2, 3)),
             dma((steps * CORES,)), dma((TRACKS,)), dma((TRACKS,)),
         ],
         compiler_params=pltpu.CompilerParams(

time: 140 us -> 136 us (0.971)
  Pallas kernels: 140 us -> 136 us
    pallas_call x1, Pallas kernels: 136 us -> 132 us  [on_device(): pl.pallas_call(functools.partial(kernel, ranks, cap), out_shape=[pltpu.VM...]
where the time goes in v5:
time: 136 us
  Pallas kernels  136 us (100%)
    pallas_call x1, Pallas kernels, on_device(): pl.pallas_call(functools.partial(kernel, ranks, cap), out_shape=[pltpu.VM...  132 us
    pallas_call x1, Pallas kernels, on_device(): pl.pallas_call(finish, out_shape=jax.ShapeDtypeStruct((units, width), BF)...  4.08 us

profile of v5, /device:TPU:1, one launch (start us, length us, event | category | flops | bytes accessed | tf_op | source)
XLA Modules:
  0.0 136.2 jit_solution(14655721910551609426)
XLA Ops:
  0.0 132.1 %shard_map.46 = (bf16[14,1280,256]{2,1,0:T(8,128)(2,1)S(1)}, bf16[2,4,4,80,256]{4,3,2,1,0:T(8,128)(2,1)S(1)}, bf16[1280,1280]{1,0:T(8,128)(2,1)S(1)}) custom-call(bf16[2,128,3584]{2,1,0:T(8,128)(2,1)} %bitcast.10, s32[2,8,128]{2,1,0:T(8,128)} %bitcast.11, s32[2,8,128]{2,1,0:T(8,128)} %bitcast.12, bf16[2,1280,1280]{2,1,0:T(8,128)(2,1)} %bitcast.9), custom_call_target="tpu_custom_call" | custom-call | tf_op jit(solution)/shard_map/pallas_call | solution.py:391
  132.1 4.1 %shard_map.47 = bf16[1280,3584]{1,0:T(8,128)(2,1)} custom-call(bf16[14,1280,256]{2,1,0:T(8,128)(2,1)S(1)} %get-tuple-element.8.total, bf16[2,4,4,80,256]{4,3,2,1,0:T(8,128)(2,1)S(1)} %get-tuple-element.9.last, bf16[1280,1280]{1,0:T(8,128)(2,1)S(1)} %get-tuple-element.10.hid_two), custom_call_target="tpu_custom_call" | custom-call | tf_op jit(solution)/shard_map/pallas_call | solution.py:426

commit v6 on v5

--- a/solution.py
+++ b/solution.py
@@ -12,10 +12,10 @@
 CORES = 2
 LANES = 128
 WIDE = 2 * LANES
-TRACKS = 3
-AHEAD = 7
-LAGS = ((0, 7, 0), (5, 2, 1), (6, 1, 2), (7, 0, 3), (9, 0, 4))
-VLIM = 46 * 1024 * 1024
+TRACKS = 4
+AHEAD = 4
+LAGS = ((0, 4, 0), (2, 2, 1), (3, 1, 2), (4, 0, 3), (6, 0, 4))
+VLIM = 48 * 1024 * 1024
 INNER = ((0, 0), (0, -1), (-1, -1), (1, 0), (1, 1), (2, 1))
 LEAVES = (((0, 1), (-1, 0)), ((0, -1), (1, 0)), ((-1, 0), (0, -1)), ((1, 0),), ((0, 1),), ((0, 1), (1, 0)))
 SIGNS = (1, -1)
@@ -40,7 +40,6 @@
     chunks = half // WIDE
     steps = 2 * chunks
     both = CORES * cap
-    piece = units // SIDE
 
     rank = lax.axis_index("pipe")
     expert = lax.axis_index("expert")
@@ -223,7 +222,7 @@
         await_bytes(full.at[s, 0, pl.ds(0, 2)], hop_sem.at[s, 2])
         await_bytes(full.at[s, 0, 0], sib_sem.at[s])
         await_bytes(full.at[s, 0, 0], own_sem.at[s])
-        for p in range(2):
+        def place(p):
             for n in range(len(INNER)):
                 rows = full[s, p, n].reshape(CORES * tokens, LANES)
                 count = 2 + CORES * len(LEAVES[n])
@@ -231,39 +230,36 @@
                               preferred_element_type=F32).astype(BF)
                 z_, y_ = origin(p, n)
 
-                @pl.when(s < steps - 1)
-                def _():
-                    tiles[s * CORES + c, z_, y_, :, p * LANES:(p + 1) * LANES] = got[:both]
-
-                @pl.when(s == steps - 1)
-                def _():
-                    last[c, z_, y_, :, p * LANES:(p + 1) * LANES] = got[:both]
-
+                tiles[lax.rem(s, steps - 1) * CORES + c, z_, y_, :, p * LANES:(p + 1) * LANES] = got[:both]
+                last[c, z_, y_, :, p * LANES:(p + 1) * LANES] = got[:both]
                 to_sib[track, p, n] = got[both:2 * both]
                 for i in range(len(LEAVES[n])):
                     for core in range(CORES):
                         at_ = (2 + CORES * i + core) * both
                         to_far[track, p, first_leaf[n] + i, core] = got[at_:at_ + both]
 
-        def hand_on(into):
-            for p, sign in enumerate(SIGNS):
-                for n in range(len(INNER)):
-                    z_, y_ = origin(p, n)
-                    part = into.at[z_, y_, :, pl.ds(p * LANES, LANES)]
-                    for i, (da, db) in enumerate(LEAVES[n]):
-                        for core in range(CORES):
-                            send(to_far.at[track, p, first_leaf[n] + i, core], part, far_send.at[track],
-                                 tile_sem.at[s * CORES + c],
-                                 at_ab(wrap(mine_a + sign * da), wrap(mine_b + sign * db), core))
-                    send(to_sib.at[track, p, n], part, sib_send.at[track], tile_sem.at[s * CORES + c], sibling)
-
-        @pl.when(s < steps - 1)
-        def _():
-            hand_on(tiles.at[s * CORES + c])
-
-        @pl.when(s == steps - 1)
-        def _():
-            hand_on(last.at[c])
+        def hand_on(into, p):
+            sign = SIGNS[p]
+            for n in range(len(INNER)):
+                z_, y_ = origin(p, n)
+                part = into.at[z_, y_, :, pl.ds(p * LANES, LANES)]
+                for i, (da, db) in enumerate(LEAVES[n]):
+                    for core in range(CORES):
+                        send(to_far.at[track, p, first_leaf[n] + i, core], part, far_send.at[track],
+                             tile_sem.at[s * CORES + c],
+                             at_ab(wrap(mine_a + sign * da), wrap(mine_b + sign * db), core))
+                send(to_sib.at[track, p, n], part, sib_send.at[track], tile_sem.at[s * CORES + c], sibling)
+
+        for p in range(2):
+            place(p)
+
+            @pl.when(s < steps - 1)
+            def _():
+                hand_on(tiles.at[s * CORES + c], p)
+
+            @pl.when(s == steps - 1)
+            def _():
+                hand_on(last.at[c], p)
 
     def stage_e(s):
         d, k = s // chunks, lax.rem(s, chunks)
@@ -275,16 +271,11 @@
             await_bytes(hid_two, xh_sem)
 
         def add_product(hid, prior):
-            @pl.loop(0, CORES)
-            def _(h):
-                @pl.loop(0, 1)
-                def _(f):
-                    rows = pl.ds(f * (units // 1), units // 1)
-                    got = jnp.dot(hid[rows, :], tiles[s * CORES + h].reshape(slots, WIDE),
-                                  preferred_element_type=F32)
-                    if prior:
-                        got = got + total[k * CORES + h, rows, :].astype(F32)
-                    total[k * CORES + h, rows, :] = got.astype(BF)
+            for h in range(CORES):
+                got = jnp.dot(hid[...], tiles[s * CORES + h].reshape(slots, WIDE), preferred_element_type=F32)
+                if prior:
+                    got = got + total[k * CORES + h].astype(F32)
+                total[k * CORES + h] = got.astype(BF)
 
         @pl.when(d == 0)
         def _():
@@ -332,7 +323,7 @@
                 (stage_a, stage_b, stage_c, stage_d, stage_e)[work](i - lag)
         return carry
 
-    lax.fori_loop(AHEAD, steps + LAGS[-1][0], turn, 0)
+    lax.fori_loop(AHEAD, steps + max(lag for lag, _, _ in LAGS), turn, 0)
 
     for track in range(TRACKS):
         await_bytes(to_far.at[track], far_send.at[track])
@@ -355,7 +346,6 @@
     count, units, wide = total.shape
     slots = hid_two.shape[1]
     chunks = count // CORES
-    piece = units // SIDE
 
     def put(k, h):
         cols = pl.ds(h * chunks * wide + k * wide, wide)
@@ -368,9 +358,10 @@
     for h in range(CORES):
         @pl.loop(0, SIDE)
         def _(f):
-            rows = pl.ds(f * piece, piece)
+            rows = pl.ds(f * (units // SIDE), units // SIDE)
             got = jnp.dot(hid_two[rows, :], last[h].reshape(slots, wide), preferred_element_type=F32)
             made[h, rows, :] = (got + total[count - CORES + h, rows, :].astype(F32)).astype(BF)
+
         put(chunks - 1, h).start()
     for k in range(chunks):
         for h in range(CORES):

time: 136 us -> 134 us (0.985)
  Pallas kernels: 136 us -> 134 us
    pallas_call x1, Pallas kernels: 132 us -> 130 us  [on_device(): pl.pallas_call(functools.partial(kernel, ranks, cap), out_shape=[pltpu.VM...]
where the time goes in v6:
time: 134 us
  Pallas kernels  134 us (100%)
    pallas_call x1, Pallas kernels, on_device(): pl.pallas_call(functools.partial(kernel, ranks, cap), out_shape=[pltpu.VM...  130 us
    pallas_call x1, Pallas kernels, on_device(): pl.pallas_call(finish, out_shape=jax.ShapeDtypeStruct((units, width), BF)...  4.08 us

profile of v6, /device:TPU:1, one launch (start us, length us, event | category | flops | bytes accessed | tf_op | source)
XLA Modules:
  0.0 133.7 jit_solution(8479028060080333355)
XLA Ops:
  0.0 129.6 %shard_map.46 = (bf16[14,1280,256]{2,1,0:T(8,128)(2,1)S(1)}, bf16[2,4,4,80,256]{4,3,2,1,0:T(8,128)(2,1)S(1)}, bf16[1280,1280]{1,0:T(8,128)(2,1)S(1)}) custom-call(bf16[2,128,3584]{2,1,0:T(8,128)(2,1)} %bitcast.10, s32[2,8,128]{2,1,0:T(8,128)} %bitcast.11, s32[2,8,128]{2,1,0:T(8,128)} %bitcast.12, bf16[2,1280,1280]{2,1,0:T(8,128)(2,1)} %bitcast.9), custom_call_target="tpu_custom_call" | custom-call | tf_op jit(solution)/shard_map/pallas_call | solution.py:382
  129.6 4.1 %shard_map.47 = bf16[1280,3584]{1,0:T(8,128)(2,1)} custom-call(bf16[14,1280,256]{2,1,0:T(8,128)(2,1)S(1)} %get-tuple-element.8.total, bf16[2,4,4,80,256]{4,3,2,1,0:T(8,128)(2,1)S(1)} %get-tuple-element.9.last, bf16[1280,1280]{1,0:T(8,128)(2,1)S(1)} %get-tuple-element.10.hid_two), custom_call_target="tpu_custom_call" | custom-call | tf_op jit(solution)/shard_map/pallas_call | solution.py:417
